TPU v7x, 32 devices: a whole 2x2x4 slice. The times are simulated.
32 devices in a mesh: ctx: 16 (over z, x, core), head: 2 (over y).
Axes of the slice: x: 2, y: 2, z: 4, core: 2. Of those that a mesh axis runs over, the one named last changes fastest.
Arguments:
- queries: bfloat16 [2048, 64, 576], P('ctx', 'head'), may hold values from -512 to 512
- latents: bfloat16 [2048, 576], P('ctx'), may hold values from -4 to 4
- index_queries: bfloat16 [2048, 64, 128], P('ctx', 'head'), may hold values from -512 to 512
- index_keys: bfloat16 [2048, 128], P('ctx'), may hold values from -4 to 4
- head_weights: float32 [2048, 64], P('ctx', 'head'), may hold values from -1.5 to 1.5
- block_pos: int32 [16], replicated, may hold values from 0 to 15, each once
Outputs:
- grad_index_queries: float32 [2048, 64, 128], P('ctx', 'head')
- grad_index_keys: float32 [2048, 128], P('ctx')
All inputs are finite; a program needn't handle non-finite values.
Results may differ from a plain program's by a relative error of at most 0.008.
Values may be sent and summed in bfloat16 or wider, within the bound.
A program may use at most 128 MiB of HBM per device.

v0:
```python
import functools
import math

import jax
import jax.numpy as jnp
from jax import lax
from jax.experimental import pallas as pl
from jax.experimental.pallas import tpu as pltpu
from jax.sharding import PartitionSpec as P

HEADS = 64
SCALE_ATTN = 192.0 ** (-0.5)
LOSS_SCALE = 1024.0
NEGATIVE = -1e30
LOG2E = math.log2(math.e)
MESH = pl.DeviceIdType.MESH
F32 = jnp.float32
BF16 = jnp.bfloat16
TOK = 8
VMEM_LIMIT = 60 * 1024 * 1024


def place(n):
    me = lax.axis_index("ctx")
    a = n // 4
    return me // 4, (me // 2) % 2, me % 2, a


def at(z, x, c):
    return (z * 2 + x) * 2 + c


def remote(src, dst, send, recv, **where):
    return pltpu.make_async_remote_copy(
        src_ref=src, dst_ref=dst, send_sem=send, recv_sem=recv, device_id=where, device_id_type=MESH
    )


def gather_kernel(n, lat_ref, key_ref, lat_out, key_out, send_sem, recv_sem, own_sem):
    z, x, c, a = place(n)
    up, down = z + 1 < a, z > 0
    barrier = pltpu.get_barrier_semaphore()

    def greet(index):
        pl.semaphore_signal(barrier, inc=1, device_id={"ctx": index}, device_id_type=MESH)

    greet(at(z, 1 - x, c))
    greet(at(z, x, 1 - c))

    @pl.when(up)
    def _():
        greet(at(z + 1, x, c))

    @pl.when(down)
    def _():
        greet(at(z - 1, x, c))

    me = at(z, x, c)
    owns = []
    for k, (src, dst) in enumerate(((key_ref, key_out), (lat_ref, lat_out))):
        own = pltpu.make_async_copy(src, dst.at[me], own_sem.at[k])
        own.start()
        owns.append(own)
    pl.semaphore_wait(barrier, 2 + up.astype(jnp.int32) + down.astype(jnp.int32))

    outs = (key_out, lat_out)
    ins = (key_ref, lat_ref)

    def copy(k, slot, way, target, first):
        src = ins[k] if first else outs[k].at[slot]
        return remote(
            src, outs[k].at[slot], send_sem.at[k, slot, way], recv_sem.at[k, slot], ctx=target
        )

    def arrived(k, slot):
        copy(k, slot, 0, at(z, x, 1 - c), False).wait_recv()

    def ways(k, zs, d, side, act):
        slot = at(zs, x, c)
        first = d == 0
        if side >= 0:

            @pl.when(up)
            def _():
                act(copy(k, slot, 2, at(z + 1, x, c), first))

        if side <= 0:

            @pl.when(down)
            def _():
                act(copy(k, slot, 3, at(z - 1, x, c), first))

        act(copy(k, slot, 1, at(z, 1 - x, c), first))
        act(copy(k, slot, 0, at(z, x, 1 - c), first))

    def each(d, side):
        zs = z - d if side >= 0 else z + d
        ok = zs >= 0 if side >= 0 else zs < a
        return zs, ok

    start = lambda item: item.start()
    done = lambda item: item.wait_send()
    for k in range(2):
        ways(k, z, 0, 0, start)
    for d in range(1, a):
        for k in range(2):
            for side in (1, -1):
                zs, ok = each(d, side)

                @pl.when(ok)
                def _():
                    arrived(k, at(zs, x, c))
                    ways(k, zs, d, side, start)

            for side in (1, -1) if d > 1 else (1,):
                zs, ok = each(d - 1, side)

                @pl.when(ok)
                def _():
                    slot = at(zs, 1 - x, c)
                    arrived(k, slot)
                    copy(k, slot, 0, at(z, x, 1 - c), False).start()

    for k in range(2):
        for side in (1, -1):
            zs, ok = each(a - 1, side)

            @pl.when(ok)
            def _():
                slot = at(zs, 1 - x, c)
                arrived(k, slot)
                copy(k, slot, 0, at(z, x, 1 - c), False).start()

    for k in range(2):
        owns[k].wait()
        for zs in range(a):
            for xs in range(2):
                arrived(k, at(zs, xs, 1 - c))
        ways(k, z, 0, 0, done)
        for d in range(1, a):
            for side in (1, -1):
                zs, ok = each(d, side)

                @pl.when(ok)
                def _():
                    ways(k, zs, d, side, done)

        for zs in range(a):
            copy(k, at(zs, 1 - x, c), 0, at(z, x, 1 - c), False).wait_send()


def gather(latents, keys, n):
    rows = latents.shape[0]
    hbm = pl.BlockSpec(memory_space=pl.ANY)
    return pl.pallas_call(
        functools.partial(gather_kernel, n),
        out_shape=(
            jax.ShapeDtypeStruct((n, rows, latents.shape[1]), BF16),
            jax.ShapeDtypeStruct((n, rows, keys.shape[1]), BF16),
        ),
        in_specs=[hbm, hbm],
        out_specs=(hbm, hbm),
        scratch_shapes=[
            pltpu.SemaphoreType.DMA((2, n, 4)),
            pltpu.SemaphoreType.DMA((2, n)),
            pltpu.SemaphoreType.DMA((2,)),
        ],
        compiler_params=pltpu.CompilerParams(collective_id=0, has_side_effects=True),
        name="gather",
    )(latents, keys)


def dot_t(a, b):
    return lax.dot_general(a, b, (((1,), (1,)), ((), ())), preferred_element_type=F32)


def index_kernel(heads, iq_ref, w_ref, key_ref, out_ref, scr):
    scr[...] = dot_t(iq_ref[...], key_ref[...])
    rows = []
    for t in range(TOK):
        acc = None
        for g in range(0, heads, 8):
            r = t * heads + g
            w = w_ref[r : r + 8, 0:1]
            part = jnp.maximum(scr[r : r + 8, :], 0.0) * w
            acc = part if acc is None else acc + part
        rows.append(jnp.sum(acc, axis=0, keepdims=True))
    out_ref[...] = jnp.concatenate(rows, axis=0)


def index_part(iq, wide, keys, heads):
    total, depth = iq.shape
    seq = keys.shape[0]
    m = TOK * heads
    return pl.pallas_call(
        functools.partial(index_kernel, heads),
        grid=(total // m,),
        out_shape=jax.ShapeDtypeStruct((total // heads, seq), F32),
        in_specs=[
            pl.BlockSpec((m, depth), lambda i: (i, 0)),
            pl.BlockSpec((m, wide.shape[1]), lambda i: (i, 0)),
            pl.BlockSpec((seq, depth), lambda i: (0, 0)),
        ],
        out_specs=pl.BlockSpec((TOK, seq), lambda i: (i, 0)),
        scratch_shapes=[pltpu.VMEM((m, seq), F32)],
        compiler_params=pltpu.CompilerParams(vmem_limit_bytes=VMEM_LIMIT),
        cost_estimate=pl.CostEstimate(
            flops=4 * total * seq * depth, bytes_accessed=4 * total * depth, transcendentals=0
        ),
        name="index_part",
    )(iq, wide, keys)


def attend_kernel(heads, q_ref, lat_ref, post_ref, poss_ref, out_ref, low_ref, scr, bias):
    scr[...] = dot_t(q_ref[...], lat_ref[...])
    bias[...] = jnp.where(poss_ref[...] <= post_ref[...], 0.0, NEGATIVE)
    rows = []
    for t in range(TOK):
        acc = None
        for g in range(0, heads, 8):
            r = t * heads + g
            s = scr[r : r + 8, :] + bias[t : t + 1, :]
            top = jnp.max(s, axis=1, keepdims=True)
            p = jnp.exp2((s - top) * (SCALE_ATTN * LOG2E))
            part = p * (1.0 / (HEADS * jnp.sum(p, axis=1, keepdims=True)))
            acc = part if acc is None else acc + part
        rows.append(jnp.sum(acc, axis=0, keepdims=True))
    out = jnp.concatenate(rows, axis=0)
    out_ref[...] = out
    low_ref[...] = out.astype(BF16)


def attend(q, lat, pos_t, pos_s, heads, first, count):
    depth = q.shape[1]
    seq = lat.shape[0]
    m = TOK * heads
    off = first // TOK
    return pl.pallas_call(
        functools.partial(attend_kernel, heads),
        grid=(count // TOK,),
        out_shape=(
            jax.ShapeDtypeStruct((count, seq), F32),
            jax.ShapeDtypeStruct((count, seq), BF16),
        ),
        in_specs=[
            pl.BlockSpec((m, depth), lambda i: (i + off, 0)),
            pl.BlockSpec((seq, depth), lambda i: (0, 0)),
            pl.BlockSpec((TOK, 1), lambda i: (i + off, 0)),
            pl.BlockSpec((1, seq), lambda i: (0, 0)),
        ],
        out_specs=(
            pl.BlockSpec((TOK, seq), lambda i: (i, 0)),
            pl.BlockSpec((TOK, seq), lambda i: (i, 0)),
        ),
        scratch_shapes=[pltpu.VMEM((m, seq), F32), pltpu.VMEM((TOK, seq), F32)],
        compiler_params=pltpu.CompilerParams(vmem_limit_bytes=VMEM_LIMIT),
        cost_estimate=pl.CostEstimate(
            flops=4 * count * heads * seq * depth,
            bytes_accessed=2 * count * heads * depth,
            transcendentals=count * heads * seq,
        ),
        name="attend",
    )(q, lat, pos_t, pos_s)


def back_kernel(heads, last, iq_ref, w_ref, key_ref, post_ref, poss_ref, *rest):
    peers_i = rest[0]
    own_i, own_t, peers_t, carry, gq_ref, gk_ref, scr, coef, acc, dscr = rest[1:]
    step = pl.program_id(0)

    @pl.when(step == 0)
    def _():
        acc[...] = carry[...]

    scr[...] = dot_t(iq_ref[...], key_ref[...])
    index, target = own_i[...], own_t[...]
    for k in range(peers_i.shape[0]):
        index = index + peers_i[k]
        target = target + peers_t[k].astype(F32)
    seen = poss_ref[...] <= post_ref[...]
    masked = jnp.where(seen, index, NEGATIVE)
    weights = jnp.where(seen, jnp.exp(masked - jnp.max(masked, axis=1, keepdims=True)), 0.0)
    prob = weights * (1.0 / jnp.sum(weights, axis=1, keepdims=True))
    dscr[...] = jnp.where(seen, LOSS_SCALE * (prob - target), 0.0).astype(BF16).astype(F32)
    for t in range(TOK):
        for g in range(0, heads, 8):
            r = t * heads + g
            value = dscr[t : t + 1, :] * w_ref[r : r + 8, 0:1]
            coef[r : r + 8, :] = jnp.where(scr[r : r + 8, :] > 0.0, value, 0.0).astype(BF16)
    gq_ref[...] = jnp.dot(coef[...], key_ref[...], preferred_element_type=F32)
    acc[...] += lax.dot_general(
        iq_ref[...], coef[...], (((0,), (0,)), ((), ())), preferred_element_type=F32
    )

    @pl.when(step == pl.num_programs(0) - 1)
    def _():
        if last:
            gk_ref[...] = jnp.transpose(acc[...]).astype(BF16)
        else:
            gk_ref[...] = acc[...]


def back(iq, wide, keys, pos_t, pos_s, peers_i, own_i, own_t, peers_t, carry, heads, first, last):
    depth = iq.shape[1]
    seq = keys.shape[0]
    count = own_t.shape[0]
    m = TOK * heads
    off = first // TOK
    others = peers_i.shape[0]
    return pl.pallas_call(
        functools.partial(back_kernel, heads, last),
        grid=(count // TOK,),
        out_shape=(
            jax.ShapeDtypeStruct((count * heads, depth), F32),
            jax.ShapeDtypeStruct((seq, depth), BF16)
            if last
            else jax.ShapeDtypeStruct((depth, seq), F32),
        ),
        in_specs=[
            pl.BlockSpec((m, depth), lambda i: (i + off, 0)),
            pl.BlockSpec((m, wide.shape[1]), lambda i: (i + off, 0)),
            pl.BlockSpec((seq, depth), lambda i: (0, 0)),
            pl.BlockSpec((TOK, 1), lambda i: (i + off, 0)),
            pl.BlockSpec((1, seq), lambda i: (0, 0)),
            pl.BlockSpec((others, TOK, seq), lambda i: (0, i + off, 0)),
            pl.BlockSpec((TOK, seq), lambda i: (i + off, 0)),
            pl.BlockSpec((TOK, seq), lambda i: (i, 0)),
            pl.BlockSpec((others, TOK, seq), lambda i: (0, i, 0)),
            pl.BlockSpec((depth, seq), lambda i: (0, 0)),
        ],
        out_specs=(
            pl.BlockSpec((m, depth), lambda i: (i, 0)),
            pl.BlockSpec((seq, depth) if last else (depth, seq), lambda i: (0, 0)),
        ),
        scratch_shapes=[
            pltpu.VMEM((m, seq), F32),
            pltpu.VMEM((m, seq), BF16),
            pltpu.VMEM((depth, seq), F32),
            pltpu.VMEM((TOK, seq), F32),
        ],
        compiler_params=pltpu.CompilerParams(vmem_limit_bytes=VMEM_LIMIT),
        cost_estimate=pl.CostEstimate(
            flops=8 * count * heads * seq * depth,
            bytes_accessed=8 * count * heads * depth,
            transcendentals=0,
        ),
        name="back",
    )(iq, wide, keys, pos_t, pos_s, peers_i, own_i, own_t, peers_t, carry)


def scatter_kernel(
    n, ranks, gk_ref, out_ref, got1, sum1, put2, got2, sum2, put3, got3, put4, got4, ssem, rsem
):
    z, x, c, a = place(n)
    y = lax.axis_index("head")
    barrier = pltpu.get_barrier_semaphore()
    greeted = [dict(ctx=at(z, 1 - x, c)), dict(ctx=at(z, x, 1 - c))]
    greeted += [dict(ctx=at(lax.rem(z + d, a), x, c)) for d in range(1, a)]
    greeted += [dict(head=lax.rem(y + d, ranks)) for d in range(1, ranks)]
    for where in greeted:
        pl.semaphore_signal(barrier, inc=1, device_id=where, device_id_type=MESH)
    pl.semaphore_wait(barrier, len(greeted))

    first = remote(gk_ref.at[:, :, 1 - c], got1, ssem.at[0], rsem.at[0], ctx=at(z, x, 1 - c))
    first.start()
    first.wait()
    sum1[...] = gk_ref[:, :, c].astype(F32) + got1[...].astype(F32)
    put2[...] = sum1[:, 1 - x].astype(BF16)
    second = remote(put2, got2, ssem.at[1], rsem.at[1], ctx=at(z, 1 - x, c))
    second.start()
    second.wait()
    sum2[...] = sum1[:, x] + got2[...].astype(F32)
    put3[...] = sum2[...].astype(BF16)
    third = []
    for d in range(1, a):
        to = lax.rem(z + d, a)
        item = remote(
            put3.at[to], got3.at[d - 1], ssem.at[1 + d], rsem.at[1 + d], ctx=at(to, x, c)
        )
        item.start()
        third.append(item)
    for item in third:
        item.wait()
    part = sum2[z]
    for d in range(1, a):
        part = part + got3[d - 1].astype(F32)
    put4[...] = part
    fourth = []
    for d in range(1, ranks):
        item = remote(
            put4,
            got4.at[d - 1],
            ssem.at[a + d],
            rsem.at[a + d],
            head=lax.rem(y + d, ranks),
        )
        item.start()
        fourth.append(item)
    for item in fourth:
        item.wait()
    part = put4[...]
    for d in range(1, ranks):
        part = part + got4[d - 1]
    out_ref[...] = part


def scatter(gk, n, ranks):
    a = n // 4
    rows, depth = gk.shape[0] // n, gk.shape[1]
    vmem = pl.BlockSpec(memory_space=pltpu.VMEM)
    return pl.pallas_call(
        functools.partial(scatter_kernel, n, ranks),
        out_shape=jax.ShapeDtypeStruct((rows, depth), F32),
        in_specs=[vmem],
        out_specs=vmem,
        scratch_shapes=[
            pltpu.VMEM((a, 2, rows, depth), BF16),
            pltpu.VMEM((a, 2, rows, depth), F32),
            pltpu.VMEM((a, rows, depth), BF16),
            pltpu.VMEM((a, rows, depth), BF16),
            pltpu.VMEM((a, rows, depth), F32),
            pltpu.VMEM((a, rows, depth), BF16),
            pltpu.VMEM((a - 1, rows, depth), BF16),
            pltpu.VMEM((rows, depth), F32),
            pltpu.VMEM((ranks - 1, rows, depth), F32),
            pltpu.SemaphoreType.DMA((a + ranks,)),
            pltpu.SemaphoreType.DMA((a + ranks,)),
        ],
        compiler_params=pltpu.CompilerParams(collective_id=1, has_side_effects=True),
        name="scatter",
    )(gk.reshape(a, 2, 2, rows, depth))


def swap(value, ranks):
    return jnp.stack(
        [
            lax.ppermute(value, "head", [(i, (i + d) % ranks) for i in range(ranks)])
            for d in range(1, ranks)
        ]
    )


def body(queries, latents, index_queries, index_keys, head_weights, block_pos):
    rows, heads, rank = queries.shape
    depth = index_queries.shape[2]
    n, ranks = lax.axis_size("ctx"), lax.axis_size("head")
    seq = rows * n
    q = queries.reshape(rows * heads, rank)
    iq = index_queries.reshape(rows * heads, depth)
    wide = jnp.broadcast_to(
        (head_weights * depth ** (-0.5))[:, :, None], (rows, heads, 128)
    ).reshape(rows * heads, 128)
    local = jnp.arange(rows, dtype=jnp.int32)
    pos_s = (block_pos[:, None] * rows + local[None, :]).reshape(1, seq)
    mine = jnp.sum(jnp.where(jnp.arange(n) == lax.axis_index("ctx"), block_pos, 0))
    pos_t = (mine * rows + local)[:, None]

    lat, keys = gather(latents, index_keys, n)
    lat = lat.reshape(seq, rank)
    keys = keys.reshape(seq, depth)
    own_i = index_part(iq, wide, keys, heads)
    peers_i = swap(own_i, ranks)
    half = rows // 2
    own_t, peers_t = [], []
    for k in range(2):
        full, low = attend(q, lat, pos_t, pos_s, heads, k * half, half)
        own_t.append(full)
        peers_t.append(swap(low, ranks))
    carry = jnp.zeros((depth, seq), F32)
    grads = []
    for k in range(2):
        gq, carry = back(
            iq, wide, keys, pos_t, pos_s, peers_i, own_i, own_t[k], peers_t[k], carry, heads,
            k * half, k == 1,
        )
        grads.append(gq)
    grad_queries = jnp.concatenate(grads, 0).reshape(rows, heads, depth)
    return grad_queries, scatter(carry, n, ranks)


def solution(mesh):
    return jax.shard_map(
        body,
        mesh=mesh,
        in_specs=(
            P("ctx", "head", None),
            P("ctx", None),
            P("ctx", "head", None),
            P("ctx", None),
            P("ctx", "head"),
            P(),
        ),
        out_specs=(P("ctx", "head", None), P("ctx", None)),
        check_vma=False,
    )
```

profile of v0, /device:TPU:0, one launch (start us, length us, event | category | flops | bytes accessed | tf_op | source)
XLA Modules:
  0.0 134.8 jit_solution(7372650885542435472)
XLA Ops:
  0.6 0.7 broadcast_multiply_fusion
  1.4 0.1 copy.10
  1.4 0.1 broadcast_in_dim.18
  1.5 1.7 %copy.11.lat_ref = bf16[128,576]{1,0:T(8,128)(2,1)} copy(bf16[128,576]{0,1:T(8,128)(2,1)} %param.7) | data formatting | bytes 294912 | tf_op args[1]
  3.3 27.7 %gather.1 = (bf16[16,128,576]{2,1,0:T(8,128)(2,1)}, bf16[16,128,128]{2,1,0:T(8,128)(2,1)}) custom-call(bf16[128,576]{1,0:T(8,128)(2,1)} %copy.11.lat_ref, bf16[128,128]{1,0:T(8,128)(2,1)} %key_ref.1), custom_call_target="tpu_custom_call" | custom-call | tf_op jit(solution)/shard_map/gather/pallas_call | solution.py:155
  30.9 1.9 %broadcast_in_dim.19.w_ref = f32[4096,128]{1,0:T(8,128)} broadcast(f32[4096]{0:T(1024)S(1)} %broadcast_in_dim.18), dimensions={0} | broadcast | bytes 2113536 | tf_op jit(solution)/shard_map/broadcast_in_dim | solution.py:450
  32.9 0.0 copy-start.2
  32.9 13.2 %index_part.1.rest_1_ = f32[128,2048]{1,0:T(8,128)} custom-call(bf16[4096,128]{1,0:T(8,128)(2,1)} %bitcast.20, f32[4096,128]{1,0:T(8,128)} %broadcast_in_dim.19.w_ref, bf16[2048,128]{1,0:T(8,128)(2,1)} %bitcast.25), custom_call_target="tpu_custom_call" | custom-call | flops 4294967296 | bytes 2097152 | tf_op jit(solution)/shard_map/index_part/pallas_call | solution.py:195
  46.1 1.5 %collective-permute-start = (f32[128,2048]{1,0:T(8,128)}, f32[128,2048]{1,0:T(8,128)S(1)}, u32[]{:S(2)}, u32[]{:S(2)}) collective-permute-start(f32[128,2048]{1,0:T(8,128)} %index_part.1.rest_1_), channel_id=1, source_target_pairs={{0,1},{1,0},{2,3},{3,2},{4,5},{5,4},{6,7},{7,6},{8,9},{9,8},{10,11... | collective-permute-start | bytes 3145736 | tf_op jit(solution)/shard_map/ppermute | solution.py:437
  47.6 0.0 copy-done.2
  47.6 0.6 broadcast_multiply_fusion.1
  48.9 0.6 iota_add_fusion.post_ref
  49.5 0.7 iota_add_fusion.1
  50.2 8.9 %copy.12 = bf16[128,32,576]{2,1,0:T(8,128)(2,1)} copy(bf16[128,32,576]{0,2,1:T(8,128)(2,1)} %param.6) | data formatting | bytes 9437184 | tf_op args[0]
  59.1 15.3 %attend.2 = (f32[64,2048]{1,0:T(8,128)}, bf16[64,2048]{1,0:T(8,128)(2,1)}) custom-call(bf16[4096,576]{1,0:T(8,128)(2,1)} %bitcast.10, bf16[2048,576]{1,0:T(8,128)(2,1)} %bitcast.18, s32[128,1]{1,0:T(8,128)} %iota_add_fusion.post_ref, s32[1,2048]{1,0:T(1,128)} %bitcast.14), custom_call_target="tpu_custom_call" | custom-call | flops 9663676416 | bytes 2359296 | tf_op jit(solution)/shard_map/attend/pallas_call | solution.py:238
  74.5 0.5 collective-permute-start.1
  75.0 15.3 %attend.3 = (f32[64,2048]{1,0:T(8,128)}, bf16[64,2048]{1,0:T(8,128)(2,1)}) custom-call(bf16[4096,576]{1,0:T(8,128)(2,1)} %bitcast.11, bf16[2048,576]{1,0:T(8,128)(2,1)} %bitcast.19, s32[128,1]{1,0:T(8,128)} %iota_add_fusion.post_ref, s32[1,2048]{1,0:T(1,128)} %bitcast.15), custom_call_target="tpu_custom_call" | custom-call | flops 9663676416 | bytes 2359296 | tf_op jit(solution)/shard_map/attend/pallas_call | solution.py:238
  90.3 1.5 %collective-permute-start.2 = (bf16[64,2048]{1,0:T(8,128)(2,1)}, bf16[64,2048]{1,0:T(8,128)(2,1)S(1)}, u32[]{:S(2)}, u32[]{:S(2)}) collective-permute-start(bf16[64,2048]{1,0:T(8,128)(2,1)} %get-tuple-element.18), channel_id=1, source_target_pairs={{0,1},{1,0},{2,3},{3,2},{4,5},{5,4},{6,7},{7,6},{8,9},{9,8},{10,11... | collective-permute-start | bytes 786440 | tf_op jit(solution)/shard_map/ppermute | solution.py:437
  91.8 0.0 collective-permute-done.1
  91.8 0.0 copy-start.5
  91.8 0.0 collective-permute-done
  91.8 0.0 copy-start.3
  91.9 1.2 broadcast_in_dim.21.rest_4_
  93.1 0.0 copy-done.5
  93.1 0.2 copy-done.3
  93.2 10.5 %back.2 = (f32[2048,128]{1,0:T(8,128)}, f32[128,2048]{1,0:T(8,128)}) custom-call(bf16[4096,128]{1,0:T(8,128)(2,1)} %bitcast.21, f32[4096,128]{1,0:T(8,128)} %broadcast_in_dim.19.w_ref, bf16[2048,128]{1,0:T(8,128)(2,1)} %bitcast.26, s32[128,1]{1,0:T(8,128)} %iota_add_fusion.post_ref, s32[1,2048]{1,0:T(1,128)} %bitcast.16, f32[1,128,2048]{2,1,0:T(8,128)} %bitcast.23, ...), custom_call_target="tpu_custom_call" | custom-call | flops 4294967296 | bytes 2097152 | tf_op jit(solution)/shard_map/back/pallas_call | solution.py:310
  103.8 0.0 collective-permute-done.2
  103.8 0.0 copy-start.4
  103.8 0.7 copy-done.4
  104.5 0.0 copy-start
  104.5 10.6 %back.3 = (f32[2048,128]{1,0:T(8,128)}, bf16[2048,128]{1,0:T(8,128)(2,1)}) custom-call(bf16[4096,128]{1,0:T(8,128)(2,1)} %bitcast.22, f32[4096,128]{1,0:T(8,128)} %broadcast_in_dim.19.w_ref, bf16[2048,128]{1,0:T(8,128)(2,1)} %bitcast.27, s32[128,1]{1,0:T(8,128)} %iota_add_fusion.post_ref, s32[1,2048]{1,0:T(1,128)} %bitcast.17, f32[1,128,2048]{2,1,0:T(8,128)} %bitcast.24, ...), custom_call_target="tpu_custom_call" | custom-call | flops 4294967296 | bytes 2097152 | tf_op jit(solution)/shard_map/back/pallas_call | solution.py:310
  115.1 16.4 %scatter.1 = f32[128,128]{1,0:T(8,128)} custom-call(bf16[4,2,2,128,128]{4,3,2,1,0:T(8,128)(2,1)} %bitcast.13), custom_call_target="tpu_custom_call" | custom-call | tf_op jit(solution)/shard_map/scatter/pallas_call | solution.py:411
  131.5 0.0 copy-done
  131.5 0.0 copy-start.1
  131.5 2.7 %pad_maximum_fusion = f32[4096,128]{1,0:T(8,128)} fusion(f32[2048,128]{1,0:T(8,128)} %get-tuple-element.20, f32[2048,128]{1,0:T(8,128)S(1)} %copy-done), kind=kLoop, calls=%fused_computation | loop fusion | flops 524288 | bytes 4194304 | tf_op jit(solution)/shard_map/concatenate | solution.py:477
  134.2 0.0 copy-done.1
  134.2 0.6 copy.14
Async XLA Ops:
  32.9 14.7 %copy-start.2 = (s32[16]{0:T(128)S(1)}, s32[16]{0:T(128)}, u32[]{:S(2)}) copy-start(s32[16]{0:T(128)} %param.11) | copy-start | bytes 196
  46.1 45.7 %collective-permute-start = (f32[128,2048]{1,0:T(8,128)}, f32[128,2048]{1,0:T(8,128)S(1)}, u32[]{:S(2)}, u32[]{:S(2)}) collective-permute-start(f32[128,2048]{1,0:T(8,128)} %index_part.1.rest_1_), channel_id=1, source_target_pairs={{0,1},{1,0},{2,3},{3,2},{4,5},{5,4},{6,7},{7,6},{8,9},{9,8},{10,11... | collective-permute-start | bytes 3145736 | tf_op jit(solution)/shard_map/ppermute | solution.py:437
  74.5 17.4 %collective-permute-start.1 = (bf16[64,2048]{1,0:T(8,128)(2,1)}, bf16[64,2048]{1,0:T(8,128)(2,1)S(1)}, u32[]{:S(2)}, u32[]{:S(2)}) collective-permute-start(bf16[64,2048]{1,0:T(8,128)(2,1)} %get-tuple-element.15), channel_id=1, source_target_pairs={{0,1},{1,0},{2,3},{3,2},{4,5},{5,4},{6,7},{7,6},{8,9},{9,8},{10,11... | collective-permute-start | bytes 786440 | tf_op jit(solution)/shard_map/ppermute | solution.py:437
  90.3 13.5 %collective-permute-start.2 = (bf16[64,2048]{1,0:T(8,128)(2,1)}, bf16[64,2048]{1,0:T(8,128)(2,1)S(1)}, u32[]{:S(2)}, u32[]{:S(2)}) collective-permute-start(bf16[64,2048]{1,0:T(8,128)(2,1)} %get-tuple-element.18), channel_id=1, source_target_pairs={{0,1},{1,0},{2,3},{3,2},{4,5},{5,4},{6,7},{7,6},{8,9},{9,8},{10,11... | collective-permute-start | bytes 786440 | tf_op jit(solution)/shard_map/ppermute | solution.py:437
  91.8 1.2 copy-start.5
  91.8 1.4 %copy-start.3 = (f32[128,2048]{1,0:T(8,128)}, f32[128,2048]{1,0:T(8,128)S(1)}, u32[]{:S(2)}) copy-start(f32[128,2048]{1,0:T(8,128)S(1)} %collective-permute-done) | copy-start | bytes 3145732
  103.8 0.7 copy-start.4
  104.5 27.0 %copy-start = (f32[2048,128]{1,0:T(8,128)S(1)}, f32[2048,128]{1,0:T(8,128)}, u32[]{:S(2)}) copy-start(f32[2048,128]{1,0:T(8,128)} %get-tuple-element.16) | copy-start | bytes 3145732
  131.5 2.7 %copy-start.1 = (f32[128,128]{1,0:T(8,128)S(1)}, f32[128,128]{1,0:T(8,128)}, u32[]{:S(2)}) copy-start(f32[128,128]{1,0:T(8,128)} %scatter.1) | copy-start | bytes 196612
where the time goes:
time: 136 us; the launch traced here: 135 us
  Pallas kernels  109 us (80%)
  local copies, waits for them, and re-layouts  15.5 us (11%)
  other arithmetic  5.37 us (4%)
  starting transfers between devices  3.55 us (3%)
  between operations  1.36 us (1%)
    pallas_call x2, Pallas kernels, attend(): pl.pallas_call(functools.partial(attend_kernel, heads), grid=(count // TO...  30.7 us
    pallas_call x1, Pallas kernels, gather(): pl.pallas_call(functools.partial(gather_kernel, n), out_shape=(jax.ShapeD...  27.7 us
    pallas_call x2, Pallas kernels, back(): pl.pallas_call(functools.partial(back_kernel, heads, last), grid=(count /...  21.1 us
    pallas_call x1, Pallas kernels, scatter(): pl.pallas_call(functools.partial(scatter_kernel, n, ranks), out_shape=jax...  16.4 us
    pallas_call x1, Pallas kernels, index_part(): pl.pallas_call(functools.partial(index_kernel, heads), grid=(total // m,)...  13.2 us
    unnamed x15, local copies, waits for them, and re-layouts  12.2 us
    ppermute x3, starting transfers between devices, swap(): lax.ppermute(value, 'head', [(i, (i + d) % ranks) for i in range(ranks)])  3.55 us
  transfers between devices with their start and end apart: 3, of which 0 were waited for; matrix products, arithmetic and copies ran while one was open for 9% of the time, Pallas kernels for 31%

commit v1 on v0

--- a/solution.py
+++ b/solution.py
@@ -211,66 +211,117 @@
     )(iq, wide, keys)
 
 
-def attend_kernel(heads, q_ref, lat_ref, post_ref, poss_ref, out_ref, low_ref, scr, bias):
-    scr[...] = dot_t(q_ref[...], lat_ref[...])
-    bias[...] = jnp.where(poss_ref[...] <= post_ref[...], 0.0, NEGATIVE)
-    rows = []
-    for t in range(TOK):
-        acc = None
-        for g in range(0, heads, 8):
-            r = t * heads + g
-            s = scr[r : r + 8, :] + bias[t : t + 1, :]
-            top = jnp.max(s, axis=1, keepdims=True)
-            p = jnp.exp2((s - top) * (SCALE_ATTN * LOG2E))
-            part = p * (1.0 / (HEADS * jnp.sum(p, axis=1, keepdims=True)))
-            acc = part if acc is None else acc + part
-        rows.append(jnp.sum(acc, axis=0, keepdims=True))
-    out = jnp.concatenate(rows, axis=0)
-    out_ref[...] = out
-    low_ref[...] = out.astype(BF16)
-
-
-def attend(q, lat, pos_t, pos_s, heads, first, count):
-    depth = q.shape[1]
+def attend_kernel(
+    half, n, q_ref, lat_ref, pos_ref, mine_ref, out_ref, low_ref, scr_a, scr_b, bias, acc
+):
+    step = pl.program_id(0)
+    seq = lat_ref.shape[0]
+    lanes = q_ref.shape[2]
+    count = lanes // 2
+    rows = seq // n
+    run = 64
+
+    @pl.when(step == 0)
+    def _():
+        lane = lax.broadcasted_iota(jnp.int32, (rows, lanes), 1)
+        row = lax.broadcasted_iota(jnp.int32, (rows, lanes), 0)
+        mine = mine_ref[0] * rows + half * count + jnp.where(lane >= count, lane - count, lane)
+        for b in range(n):
+            seen = pos_ref[b] * rows + row <= mine
+            bias[b * rows : (b + 1) * rows, :] = jnp.where(seen, 0.0, NEGATIVE)
+
+    def scores(first):
+        def part(h):
+            return q_ref[h][:, half * count : (half + 1) * count]
+
+        weights = jnp.concatenate([part(first + h) for h in range(4)], axis=1)
+        return jnp.dot(lat_ref[...], weights, preferred_element_type=F32)
+
+    def softmax(scr):
+        scale = []
+        for tile in (slice(0, lanes), slice(lanes, 2 * lanes)):
+            top = None
+            for r in range(0, seq, run):
+                v = scr[r : r + run, tile] + bias[r : r + run, :]
+                top = v if top is None else jnp.maximum(top, v)
+            top = jnp.max(top, axis=0, keepdims=True)
+            total = None
+            for r in range(0, seq, run):
+                v = scr[r : r + run, tile] + bias[r : r + run, :]
+                p = jnp.exp2((v - top) * (SCALE_ATTN * LOG2E))
+                scr[r : r + run, tile] = p
+                total = p if total is None else total + p
+            total = jnp.sum(total, axis=0, keepdims=True)
+            scale.append(1.0 / (HEADS * total))
+        for r in range(0, seq, run):
+            acc[r : r + run, :] += (
+                scr[r : r + run, :lanes] * scale[0] + scr[r : r + run, lanes:] * scale[1]
+            )
+
+    scr_a[...] = scores(0)
+    softmax(scr_b)
+
+    @pl.when(step == 0)
+    def _():
+        acc[...] = jnp.zeros_like(acc)
+
+    scr_b[...] = scores(4)
+    softmax(scr_a)
+
+    @pl.when(step == pl.num_programs(0) - 1)
+    def _():
+        softmax(scr_b)
+        both = jnp.transpose(acc[...])
+        out = both[:count] + both[count:]
+        out_ref[...] = out
+        low_ref[...] = out.astype(BF16)
+
+
+def attend(q, lat, block_pos, mine, half, n):
+    heads, depth, lanes = q.shape
     seq = lat.shape[0]
-    m = TOK * heads
-    off = first // TOK
+    count = lanes // 2
+    smem = pl.BlockSpec(memory_space=pltpu.SMEM)
+    whole = lambda i: (0, 0)
     return pl.pallas_call(
-        functools.partial(attend_kernel, heads),
-        grid=(count // TOK,),
+        functools.partial(attend_kernel, half, n),
+        grid=(heads // 8,),
         out_shape=(
             jax.ShapeDtypeStruct((count, seq), F32),
             jax.ShapeDtypeStruct((count, seq), BF16),
         ),
         in_specs=[
-            pl.BlockSpec((m, depth), lambda i: (i + off, 0)),
-            pl.BlockSpec((seq, depth), lambda i: (0, 0)),
-            pl.BlockSpec((TOK, 1), lambda i: (i + off, 0)),
-            pl.BlockSpec((1, seq), lambda i: (0, 0)),
+            pl.BlockSpec((8, depth, lanes), lambda i: (i, 0, 0)),
+            pl.BlockSpec((seq, depth), whole),
+            smem,
+            smem,
         ],
-        out_specs=(
-            pl.BlockSpec((TOK, seq), lambda i: (i, 0)),
-            pl.BlockSpec((TOK, seq), lambda i: (i, 0)),
-        ),
-        scratch_shapes=[pltpu.VMEM((m, seq), F32), pltpu.VMEM((TOK, seq), F32)],
+        out_specs=(pl.BlockSpec((count, seq), whole), pl.BlockSpec((count, seq), whole)),
+        scratch_shapes=[
+            pltpu.VMEM((seq, 2 * lanes), F32),
+            pltpu.VMEM((seq, 2 * lanes), F32),
+            pltpu.VMEM((seq, lanes), F32),
+            pltpu.VMEM((seq, lanes), F32),
+        ],
         compiler_params=pltpu.CompilerParams(vmem_limit_bytes=VMEM_LIMIT),
         cost_estimate=pl.CostEstimate(
             flops=4 * count * heads * seq * depth,
-            bytes_accessed=2 * count * heads * depth,
+            bytes_accessed=4 * count * heads * depth,
             transcendentals=count * heads * seq,
         ),
         name="attend",
-    )(q, lat, pos_t, pos_s)
+    )(q, lat, block_pos, mine)
 
 
 def back_kernel(heads, last, iq_ref, w_ref, key_ref, post_ref, poss_ref, *rest):
     peers_i = rest[0]
-    own_i, own_t, peers_t, carry, gq_ref, gk_ref, scr, coef, acc, dscr = rest[1:]
+    own_i, own_t, peers_t = rest[1:4]
+    gq_ref, gk_ref, scr, coef, acc, dscr = rest[-6:]
     step = pl.program_id(0)
 
     @pl.when(step == 0)
     def _():
-        acc[...] = carry[...]
+        acc[...] = rest[4][...] if last else jnp.zeros_like(acc)
 
     scr[...] = dot_t(iq_ref[...], key_ref[...])
     index, target = own_i[...], own_t[...]
@@ -300,7 +351,7 @@
             gk_ref[...] = acc[...]
 
 
-def back(iq, wide, keys, pos_t, pos_s, peers_i, own_i, own_t, peers_t, carry, heads, first, last):
+def back(iq, wide, keys, pos_t, pos_s, peers_i, own_i, own_t, peers_t, carried, heads, first, last):
     depth = iq.shape[1]
     seq = keys.shape[0]
     count = own_t.shape[0]
@@ -311,7 +362,7 @@
         functools.partial(back_kernel, heads, last),
         grid=(count // TOK,),
         out_shape=(
-            jax.ShapeDtypeStruct((count * heads, depth), F32),
+            jax.ShapeDtypeStruct(iq.shape, F32),
             jax.ShapeDtypeStruct((seq, depth), BF16)
             if last
             else jax.ShapeDtypeStruct((depth, seq), F32),
@@ -326,10 +377,11 @@
             pl.BlockSpec((TOK, seq), lambda i: (i + off, 0)),
             pl.BlockSpec((TOK, seq), lambda i: (i, 0)),
             pl.BlockSpec((others, TOK, seq), lambda i: (0, i, 0)),
-            pl.BlockSpec((depth, seq), lambda i: (0, 0)),
-        ],
+        ]
+        + [pl.BlockSpec((depth, seq), lambda i: (0, 0)), pl.BlockSpec(memory_space=pl.ANY)] * last,
+        input_output_aliases={10: 0} if last else {},
         out_specs=(
-            pl.BlockSpec((m, depth), lambda i: (i, 0)),
+            pl.BlockSpec((m, depth), lambda i: (i + off, 0)),
             pl.BlockSpec((seq, depth) if last else (depth, seq), lambda i: (0, 0)),
         ),
         scratch_shapes=[
@@ -345,7 +397,7 @@
             transcendentals=0,
         ),
         name="back",
-    )(iq, wide, keys, pos_t, pos_s, peers_i, own_i, own_t, peers_t, carry)
+    )(iq, wide, keys, pos_t, pos_s, peers_i, own_i, own_t, peers_t, *carried)
 
 
 def scatter_kernel(
@@ -445,7 +497,7 @@
     depth = index_queries.shape[2]
     n, ranks = lax.axis_size("ctx"), lax.axis_size("head")
     seq = rows * n
-    q = queries.reshape(rows * heads, rank)
+    q = jnp.transpose(queries, (1, 2, 0))
     iq = index_queries.reshape(rows * heads, depth)
     wide = jnp.broadcast_to(
         (head_weights * depth ** (-0.5))[:, :, None], (rows, heads, 128)
@@ -460,22 +512,19 @@
     keys = keys.reshape(seq, depth)
     own_i = index_part(iq, wide, keys, heads)
     peers_i = swap(own_i, ranks)
-    half = rows // 2
     own_t, peers_t = [], []
     for k in range(2):
-        full, low = attend(q, lat, pos_t, pos_s, heads, k * half, half)
+        full, low = attend(q, lat, block_pos, mine[None], k, n)
         own_t.append(full)
         peers_t.append(swap(low, ranks))
-    carry = jnp.zeros((depth, seq), F32)
-    grads = []
+    grads = ()
     for k in range(2):
-        gq, carry = back(
-            iq, wide, keys, pos_t, pos_s, peers_i, own_i, own_t[k], peers_t[k], carry, heads,
-            k * half, k == 1,
+        grad_queries, carry = back(
+            iq, wide, keys, pos_t, pos_s, peers_i, own_i, own_t[k], peers_t[k], grads, heads,
+            k * (rows // 2), k == 1,
         )
-        grads.append(gq)
-    grad_queries = jnp.concatenate(grads, 0).reshape(rows, heads, depth)
-    return grad_queries, scatter(carry, n, ranks)
+        grads = (carry, grad_queries)
+    return grad_queries.reshape(rows, heads, depth), scatter(carry, n, ranks)
 
 
 def solution(mesh):

time: 136 us -> 142 us (1.044)
  Pallas kernels: 109 us -> 126 us
  local copies, waits for them, and re-layouts: 15.5 us -> 7.07 us
  other arithmetic: 5.37 us -> 2.61 us
    pallas_call x2, Pallas kernels: 30.7 us -> 48.4 us  [attend(): pl.pallas_call(functools.partial(attend_kernel, half, n), grid=(heads //...]
    unnamed x15 -> x10, local copies, waits for them, and re-layouts: 12.2 us -> 4.95 us
    concatenate x1 -> x0, other arithmetic: 2.71 us -> none  [body(): grad_queries = jnp.concatenate(grads, 0).reshape(rows, heads, depth)]
  transfers between devices with their start and end apart: 3 -> 3, of which waited for: 0 -> 0; matrix products, arithmetic and copies ran while one was open for 9% -> 2% of each run, Pallas kernels for 31% -> 34%
where the time goes in v1:
time: 142 us; the launch traced here: 141 us
  Pallas kernels  126 us (89%)
  local copies, waits for them, and re-layouts  7.07 us (5%)
  starting transfers between devices  3.55 us (2%)
  other arithmetic  2.61 us (2%)
    pallas_call x2, Pallas kernels, attend(): pl.pallas_call(functools.partial(attend_kernel, half, n), grid=(heads //...  48.4 us
    pallas_call x1, Pallas kernels, gather(): pl.pallas_call(functools.partial(gather_kernel, n), out_shape=(jax.ShapeD...  27.7 us
    pallas_call x2, Pallas kernels, back(): pl.pallas_call(functools.partial(back_kernel, heads, last), grid=(count /...  20.8 us
    pallas_call x1, Pallas kernels, scatter(): pl.pallas_call(functools.partial(scatter_kernel, n, ranks), out_shape=jax...  16.4 us
    pallas_call x1, Pallas kernels, index_part(): pl.pallas_call(functools.partial(index_kernel, heads), grid=(total // m,)...  13.2 us
    unnamed x10, local copies, waits for them, and re-layouts  4.95 us
    ppermute x3, starting transfers between devices, swap(): lax.ppermute(value, 'head', [(i, (i + d) % ranks) for i in range(ranks)])  3.55 us
  transfers between devices with their start and end apart: 3, of which 0 were waited for; matrix products, arithmetic and copies ran while one was open for 2% of the time, Pallas kernels for 34%

profile of v1, /device:TPU:0, one launch (start us, length us, event | category | flops | bytes accessed | tf_op | source)
XLA Modules:
  0.0 141.0 jit_solution(4647897899688811319)
XLA Ops:
  0.6 1.7 %copy.11.lat_ref = bf16[128,576]{1,0:T(8,128)(2,1)} copy(bf16[128,576]{0,1:T(8,128)(2,1)} %param.7) | data formatting | bytes 294912 | tf_op args[1]
  2.3 1.3 broadcast_multiply_fusion.1
  3.6 27.7 %gather.1 = (bf16[16,128,576]{2,1,0:T(8,128)(2,1)}, bf16[16,128,128]{2,1,0:T(8,128)(2,1)}) custom-call(bf16[128,576]{1,0:T(8,128)(2,1)} %copy.11.lat_ref, bf16[128,128]{1,0:T(8,128)(2,1)} %key_ref.1), custom_call_target="tpu_custom_call" | custom-call | tf_op jit(solution)/shard_map/gather/pallas_call | solution.py:155
  31.3 0.0 copy-start
  31.3 24.2 %attend.3 = (f32[64,2048]{1,0:T(8,128)}, bf16[64,2048]{1,0:T(8,128)(2,1)}) custom-call(bf16[32,576,128]{2,1,0:T(8,128)(2,1)} %bitcast.14, bf16[2048,576]{1,0:T(8,128)(2,1)} %bitcast.16, s32[16]{0:T(128)} %pos_ref.3, s32[1]{0:T(128)} %bitcast.6.mine_ref), custom_call_target="tpu_custom_call" | custom-call | flops 9663676416 | bytes 4718592 | tf_op jit(solution)/shard_map/attend/pallas_call | solution.py:286
  55.5 1.5 %collective-permute-start.2 = (bf16[64,2048]{1,0:T(8,128)(2,1)}, bf16[64,2048]{1,0:T(8,128)(2,1)S(1)}, u32[]{:S(2)}, u32[]{:S(2)}) collective-permute-start(bf16[64,2048]{1,0:T(8,128)(2,1)} %get-tuple-element.17), channel_id=1, source_target_pairs={{0,1},{1,0},{2,3},{3,2},{4,5},{5,4},{6,7},{7,6},{8,9},{9,8},{10,11... | collective-permute-start | bytes 786440 | tf_op jit(solution)/shard_map/ppermute | solution.py:489
  57.0 0.0 copy-done
  57.1 0.1 copy.10
  57.2 0.1 broadcast_in_dim.10
  57.2 1.9 %broadcast_in_dim.20.w_ref = f32[4096,128]{1,0:T(8,128)} broadcast(f32[4096]{0:T(1024)S(1)} %broadcast_in_dim.10), dimensions={0} | broadcast | bytes 2113536 | tf_op jit(solution)/shard_map/broadcast_in_dim | solution.py:502
  59.2 13.2 %index_part.1.rest_1_ = f32[128,2048]{1,0:T(8,128)} custom-call(bf16[4096,128]{1,0:T(8,128)(2,1)} %bitcast.18, f32[4096,128]{1,0:T(8,128)} %broadcast_in_dim.20.w_ref, bf16[2048,128]{1,0:T(8,128)(2,1)} %bitcast.23), custom_call_target="tpu_custom_call" | custom-call | flops 4294967296 | bytes 2097152 | tf_op jit(solution)/shard_map/index_part/pallas_call | solution.py:195
  72.4 0.5 collective-permute-start
  72.9 24.2 %attend.2 = (f32[64,2048]{1,0:T(8,128)}, bf16[64,2048]{1,0:T(8,128)(2,1)}) custom-call(bf16[32,576,128]{2,1,0:T(8,128)(2,1)} %bitcast.15, bf16[2048,576]{1,0:T(8,128)(2,1)} %bitcast.17, s32[16]{0:T(128)} %pos_ref.3, s32[1]{0:T(128)} %bitcast.6.mine_ref), custom_call_target="tpu_custom_call" | custom-call | flops 9663676416 | bytes 4718592 | tf_op jit(solution)/shard_map/attend/pallas_call | solution.py:286
  97.1 1.5 %collective-permute-start.1 = (bf16[64,2048]{1,0:T(8,128)(2,1)}, bf16[64,2048]{1,0:T(8,128)(2,1)S(1)}, u32[]{:S(2)}, u32[]{:S(2)}) collective-permute-start(bf16[64,2048]{1,0:T(8,128)(2,1)} %get-tuple-element.15), channel_id=1, source_target_pairs={{0,1},{1,0},{2,3},{3,2},{4,5},{5,4},{6,7},{7,6},{8,9},{9,8},{10,11... | collective-permute-start | bytes 786440 | tf_op jit(solution)/shard_map/ppermute | solution.py:489
  99.3 0.6 iota_add_fusion.post_ref
  99.9 0.7 iota_add_fusion.1
  100.6 0.0 collective-permute-done.2
  100.6 0.0 copy-start.2
  100.6 0.0 collective-permute-done
  100.6 0.0 copy-start.1
  100.6 0.7 copy-done.2
  101.3 0.4 copy-done.1
  101.6 10.2 %back.2 = (f32[4096,128]{1,0:T(8,128)}, f32[128,2048]{1,0:T(8,128)}) custom-call(bf16[4096,128]{1,0:T(8,128)(2,1)} %bitcast.19, f32[4096,128]{1,0:T(8,128)} %broadcast_in_dim.20.w_ref, bf16[2048,128]{1,0:T(8,128)(2,1)} %bitcast.24, s32[128,1]{1,0:T(8,128)} %iota_add_fusion.post_ref, s32[1,2048]{1,0:T(1,128)} %bitcast.12, f32[1,128,2048]{2,1,0:T(8,128)} %bitcast.21, ...), custom_call_target="tpu_custom_call" | custom-call | flops 4294967296 | bytes 2097152 | tf_op jit(solution)/shard_map/back/pallas_call | solution.py:361
  111.9 0.0 collective-permute-done.1
  111.9 0.0 copy-start.3
  111.9 0.7 copy-done.3
  112.6 10.5 %back.3 = (f32[4096,128]{1,0:T(8,128)}, bf16[2048,128]{1,0:T(8,128)(2,1)}) custom-call(bf16[4096,128]{1,0:T(8,128)(2,1)} %bitcast.20, f32[4096,128]{1,0:T(8,128)} %broadcast_in_dim.20.w_ref, bf16[2048,128]{1,0:T(8,128)(2,1)} %bitcast.25, s32[128,1]{1,0:T(8,128)} %iota_add_fusion.post_ref, s32[1,2048]{1,0:T(1,128)} %bitcast.13, ...), custom_call_target="tpu_custom_call", output_to_operand_aliasing={{0}: (10, {})} | custom-call | flops 4294967296 | bytes 2097152 | tf_op jit(solution)/shard_map/back/pallas_call | solution.py:361
  123.1 16.4 %scatter.1 = f32[128,128]{1,0:T(8,128)} custom-call(bf16[4,2,2,128,128]{4,3,2,1,0:T(8,128)(2,1)} %bitcast.11), custom_call_target="tpu_custom_call" | custom-call | tf_op jit(solution)/shard_map/scatter/pallas_call | solution.py:463
  139.6 1.5 %copy.14 = f32[128,128]{1,0:T(8,128)} copy(f32[128,128]{1,0:T(8,128)} %scatter.1) | data formatting | bytes 131072
  (1 shorter events, 0.0 us)
Async XLA Ops:
  31.3 25.7 %copy-start = (f32[128,32]{0,1:T(8,128)S(1)}, f32[128,32]{0,1:T(8,128)}, u32[]{:S(2)}) copy-start(f32[128,32]{0,1:T(8,128)} %param.10) | copy-start | bytes 49156
  55.5 45.0 %collective-permute-start.2 = (bf16[64,2048]{1,0:T(8,128)(2,1)}, bf16[64,2048]{1,0:T(8,128)(2,1)S(1)}, u32[]{:S(2)}, u32[]{:S(2)}) collective-permute-start(bf16[64,2048]{1,0:T(8,128)(2,1)} %get-tuple-element.17), channel_id=1, source_target_pairs={{0,1},{1,0},{2,3},{3,2},{4,5},{5,4},{6,7},{7,6},{8,9},{9,8},{10,11... | collective-permute-start | bytes 786440 | tf_op jit(solution)/shard_map/ppermute | solution.py:489
  72.4 28.2 %collective-permute-start = (f32[128,2048]{1,0:T(8,128)}, f32[128,2048]{1,0:T(8,128)S(1)}, u32[]{:S(2)}, u32[]{:S(2)}) collective-permute-start(f32[128,2048]{1,0:T(8,128)} %index_part.1.rest_1_), channel_id=1, source_target_pairs={{0,1},{1,0},{2,3},{3,2},{4,5},{5,4},{6,7},{7,6},{8,9},{9,8},{10,11... | collective-permute-start | bytes 3145736 | tf_op jit(solution)/shard_map/ppermute | solution.py:489
  97.1 14.8 %collective-permute-start.1 = (bf16[64,2048]{1,0:T(8,128)(2,1)}, bf16[64,2048]{1,0:T(8,128)(2,1)S(1)}, u32[]{:S(2)}, u32[]{:S(2)}) collective-permute-start(bf16[64,2048]{1,0:T(8,128)(2,1)} %get-tuple-element.15), channel_id=1, source_target_pairs={{0,1},{1,0},{2,3},{3,2},{4,5},{5,4},{6,7},{7,6},{8,9},{9,8},{10,11... | collective-permute-start | bytes 786440 | tf_op jit(solution)/shard_map/ppermute | solution.py:489
  100.6 0.7 copy-start.2
  100.6 1.1 copy-start.1
  111.9 0.7 copy-start.3

commit v2 on v1

--- a/solution.py
+++ b/solution.py
@@ -17,6 +17,8 @@
 F32 = jnp.float32
 BF16 = jnp.bfloat16
 TOK = 8
+ITOK = 8
+PIECES = 8
 VMEM_LIMIT = 60 * 1024 * 1024
 
 
@@ -36,24 +38,35 @@
     )
 
 
-def gather_kernel(n, lat_ref, key_ref, lat_out, key_out, send_sem, recv_sem, own_sem):
+def dot_t(a, b):
+    return lax.dot_general(a, b, (((1,), (1,)), ((), ())), preferred_element_type=F32)
+
+
+def gather_kernel(
+    n, heads, lat_ref, key_ref, iq_ref, w_ref, lat_out, key_out, idx_ref,
+    scr_a, scr_b, send_sem, recv_sem, own_sem,
+):
     z, x, c, a = place(n)
+    y = lax.axis_index("head")
+    other_y = y + 1 - 2 * (y % 2)
     up, down = z + 1 < a, z > 0
+    partner = at(z, x, 1 - c)
     barrier = pltpu.get_barrier_semaphore()
 
-    def greet(index):
-        pl.semaphore_signal(barrier, inc=1, device_id={"ctx": index}, device_id_type=MESH)
-
-    greet(at(z, 1 - x, c))
-    greet(at(z, x, 1 - c))
+    def greet(**where):
+        pl.semaphore_signal(barrier, inc=1, device_id=where, device_id_type=MESH)
+
+    greet(ctx=at(z, 1 - x, c))
+    greet(ctx=partner)
+    greet(head=other_y)
 
     @pl.when(up)
     def _():
-        greet(at(z + 1, x, c))
+        greet(ctx=at(z + 1, x, c))
 
     @pl.when(down)
     def _():
-        greet(at(z - 1, x, c))
+        greet(ctx=at(z - 1, x, c))
 
     me = at(z, x, c)
     owns = []
@@ -61,154 +74,185 @@
         own = pltpu.make_async_copy(src, dst.at[me], own_sem.at[k])
         own.start()
         owns.append(own)
-    pl.semaphore_wait(barrier, 2 + up.astype(jnp.int32) + down.astype(jnp.int32))
-
-    outs = (key_out, lat_out)
-    ins = (key_ref, lat_ref)
-
-    def copy(k, slot, way, target, first):
-        src = ins[k] if first else outs[k].at[slot]
-        return remote(
-            src, outs[k].at[slot], send_sem.at[k, slot, way], recv_sem.at[k, slot], ctx=target
-        )
+    pl.semaphore_wait(barrier, 3 + up.astype(jnp.int32) + down.astype(jnp.int32))
+
+    rows = lat_ref.shape[0]
+    part = rows // 2
+
+    def piece(ref, k):
+        return ref.at[pl.ds(pl.multiple_of((k - 1) * part, part), part)]
+
+    def copy(k, slot, way, first, **where):
+        if isinstance(k, int) and k == 0:
+            src, dst = (key_ref if first else key_out.at[slot]), key_out.at[slot]
+        else:
+            dst = piece(lat_out.at[slot], k)
+            src = piece(lat_ref, k) if first else dst
+        return remote(src, dst, send_sem.at[k, slot, way], recv_sem.at[k, slot], **where)
+
+    def to_core(k, slot, first=False):
+        return copy(k, slot, 0, first, ctx=partner)
+
+    def to_x(k, slot, first=False):
+        return copy(k, slot, 1, first, ctx=at(z, 1 - x, c))
+
+    def to_y(k, slot):
+        return copy(k, slot, 4, False, head=other_y)
 
     def arrived(k, slot):
-        copy(k, slot, 0, at(z, x, 1 - c), False).wait_recv()
-
-    def ways(k, zs, d, side, act):
-        slot = at(zs, x, c)
-        first = d == 0
+        to_core(k, slot).wait_recv()
+
+    def line(k, slot, first, side, act):
         if side >= 0:
 
             @pl.when(up)
             def _():
-                act(copy(k, slot, 2, at(z + 1, x, c), first))
+                act(copy(k, slot, 2, first, ctx=at(z + 1, x, c)))
 
         if side <= 0:
 
             @pl.when(down)
             def _():
-                act(copy(k, slot, 3, at(z - 1, x, c), first))
-
-        act(copy(k, slot, 1, at(z, 1 - x, c), first))
-        act(copy(k, slot, 0, at(z, x, 1 - c), first))
-
-    def each(d, side):
-        zs = z - d if side >= 0 else z + d
-        ok = zs >= 0 if side >= 0 else zs < a
-        return zs, ok
+                act(copy(k, slot, 3, first, ctx=at(z - 1, x, c)))
+
+    def sides(d, act):
+        for side in (1, -1) if d > 0 else (0,):
+            zs = z - d if side >= 0 else z + d
+            if d == 0:
+                act(zs, side)
+            else:
+                ok = zs >= 0 if side > 0 else zs < a
+                pl.when(ok)(functools.partial(act, zs, side))
 
     start = lambda item: item.start()
     done = lambda item: item.wait_send()
-    for k in range(2):
-        ways(k, z, 0, 0, start)
+    mine, others = 1 + y % 2, 2 - y % 2
+
+    def column(ks, d, wait, act):
+        def go(zs, side):
+            slot = at(zs, x, c)
+            for k in ks:
+                if wait and d > 0:
+                    arrived(k, slot)
+                line(k, slot, d == 0, side, act)
+            crossing = 0 if ks == (0,) else mine
+            act(to_x(crossing, slot, d == 0))
+            for k in ks:
+                act(to_core(k, slot, d == 0))
+
+        sides(d, go)
+
+    def crossed(k, d, wait, act, onward):
+        def go(zs, side):
+            slot = at(zs, 1 - x, c)
+            if wait:
+                arrived(k, slot)
+            if onward:
+                act(to_y(k, slot))
+            act(to_core(k, slot))
+
+        sides(d, go)
+
+    column((0,), 0, True, start)
+    column((1, 2), 0, True, start)
     for d in range(1, a):
-        for k in range(2):
-            for side in (1, -1):
-                zs, ok = each(d, side)
-
-                @pl.when(ok)
-                def _():
-                    arrived(k, at(zs, x, c))
-                    ways(k, zs, d, side, start)
-
-            for side in (1, -1) if d > 1 else (1,):
-                zs, ok = each(d - 1, side)
-
-                @pl.when(ok)
-                def _():
-                    slot = at(zs, 1 - x, c)
-                    arrived(k, slot)
-                    copy(k, slot, 0, at(z, x, 1 - c), False).start()
-
-    for k in range(2):
-        for side in (1, -1):
-            zs, ok = each(a - 1, side)
-
-            @pl.when(ok)
-            def _():
-                slot = at(zs, 1 - x, c)
-                arrived(k, slot)
-                copy(k, slot, 0, at(z, x, 1 - c), False).start()
-
-    for k in range(2):
-        owns[k].wait()
-        for zs in range(a):
-            for xs in range(2):
+        column((0,), d, True, start)
+        crossed(0, d - 1, True, start, False)
+    crossed(0, a - 1, True, start, False)
+
+    owns[0].wait()
+    for zs in range(a):
+        for xs in range(2):
+            arrived(0, at(zs, xs, 1 - c))
+
+    def stage(d):
+        if d < a:
+            column((1, 2), d, True, start)
+        if 1 <= d <= a:
+            crossed(mine, d - 1, True, start, True)
+        if 2 <= d:
+            crossed(others, d - 2, True, start, False)
+
+    depth = iq_ref.shape[1]
+    m = ITOK * heads
+    width = 4 * rows
+
+    def index_chunk(i, _):
+        iq = iq_ref[pl.ds(pl.multiple_of(i * m, m), m), :]
+        w = w_ref.at[pl.ds(pl.multiple_of(i * m, m), m)]
+        out = idx_ref.at[pl.ds(pl.multiple_of(i * ITOK, ITOK), ITOK)]
+        scrs = (scr_a, scr_b)
+
+        def reduce(p):
+            scr = scrs[p % 2]
+            sums = []
+            for t in range(ITOK):
+                acc = None
+                for g in range(0, heads, 8):
+                    r = t * heads + g
+                    term = jnp.maximum(scr[r : r + 8, :], 0.0) * w[r : r + 8, 0:1]
+                    acc = term if acc is None else acc + term
+                sums.append(jnp.sum(acc, axis=0, keepdims=True))
+            out[:, p * width : (p + 1) * width] = jnp.concatenate(sums, axis=0)
+
+        count = n * rows // width
+        per = width // rows
+        for p in range(count):
+            held = key_out[p * per : (p + 1) * per].reshape(width, depth)
+            scrs[p % 2][...] = dot_t(iq, held)
+            if p > 0:
+                reduce(p - 1)
+        reduce(count - 1)
+        return 0
+
+    chunks = iq_ref.shape[0] // m
+    cut = [chunks * d // (a + 2) for d in range(a + 3)]
+    for d in range(a + 2):
+        lax.fori_loop(cut[d], cut[d + 1], index_chunk, 0)
+        if d + 1 < a + 2:
+            stage(d + 1)
+
+    owns[1].wait()
+    for zs in range(a):
+        for xs in range(2):
+            for k in (1, 2):
                 arrived(k, at(zs, xs, 1 - c))
-        ways(k, z, 0, 0, done)
-        for d in range(1, a):
-            for side in (1, -1):
-                zs, ok = each(d, side)
-
-                @pl.when(ok)
-                def _():
-                    ways(k, zs, d, side, done)
-
-        for zs in range(a):
-            copy(k, at(zs, 1 - x, c), 0, at(z, x, 1 - c), False).wait_send()
-
-
-def gather(latents, keys, n):
+    for ks in ((0,), (1, 2)):
+        for d in range(a):
+            column(ks, d, False, done)
+    for d in range(a):
+        crossed(0, d, False, done, False)
+        crossed(mine, d, False, done, True)
+        crossed(others, d, False, done, False)
+
+
+def gather(latents, keys, iq, wide, heads, n):
     rows = latents.shape[0]
+    seq = rows * n
     hbm = pl.BlockSpec(memory_space=pl.ANY)
+    vmem = pl.BlockSpec(memory_space=pltpu.VMEM)
+    m = ITOK * heads
     return pl.pallas_call(
-        functools.partial(gather_kernel, n),
+        functools.partial(gather_kernel, n, heads),
         out_shape=(
             jax.ShapeDtypeStruct((n, rows, latents.shape[1]), BF16),
             jax.ShapeDtypeStruct((n, rows, keys.shape[1]), BF16),
-        ),
-        in_specs=[hbm, hbm],
-        out_specs=(hbm, hbm),
+            jax.ShapeDtypeStruct((iq.shape[0] // heads, seq), F32),
+        ),
+        in_specs=[hbm, hbm, vmem, vmem],
+        out_specs=(hbm, vmem, vmem),
         scratch_shapes=[
-            pltpu.SemaphoreType.DMA((2, n, 4)),
-            pltpu.SemaphoreType.DMA((2, n)),
+            pltpu.VMEM((m, 4 * rows), F32),
+            pltpu.VMEM((m, 4 * rows), F32),
+            pltpu.SemaphoreType.DMA((3, n, 5)),
+            pltpu.SemaphoreType.DMA((3, n)),
             pltpu.SemaphoreType.DMA((2,)),
         ],
-        compiler_params=pltpu.CompilerParams(collective_id=0, has_side_effects=True),
+        compiler_params=pltpu.CompilerParams(
+            collective_id=0, has_side_effects=True, vmem_limit_bytes=VMEM_LIMIT
+        ),
         name="gather",
-    )(latents, keys)
-
-
-def dot_t(a, b):
-    return lax.dot_general(a, b, (((1,), (1,)), ((), ())), preferred_element_type=F32)
-
-
-def index_kernel(heads, iq_ref, w_ref, key_ref, out_ref, scr):
-    scr[...] = dot_t(iq_ref[...], key_ref[...])
-    rows = []
-    for t in range(TOK):
-        acc = None
-        for g in range(0, heads, 8):
-            r = t * heads + g
-            w = w_ref[r : r + 8, 0:1]
-            part = jnp.maximum(scr[r : r + 8, :], 0.0) * w
-            acc = part if acc is None else acc + part
-        rows.append(jnp.sum(acc, axis=0, keepdims=True))
-    out_ref[...] = jnp.concatenate(rows, axis=0)
-
-
-def index_part(iq, wide, keys, heads):
-    total, depth = iq.shape
-    seq = keys.shape[0]
-    m = TOK * heads
-    return pl.pallas_call(
-        functools.partial(index_kernel, heads),
-        grid=(total // m,),
-        out_shape=jax.ShapeDtypeStruct((total // heads, seq), F32),
-        in_specs=[
-            pl.BlockSpec((m, depth), lambda i: (i, 0)),
-            pl.BlockSpec((m, wide.shape[1]), lambda i: (i, 0)),
-            pl.BlockSpec((seq, depth), lambda i: (0, 0)),
-        ],
-        out_specs=pl.BlockSpec((TOK, seq), lambda i: (i, 0)),
-        scratch_shapes=[pltpu.VMEM((m, seq), F32)],
-        compiler_params=pltpu.CompilerParams(vmem_limit_bytes=VMEM_LIMIT),
-        cost_estimate=pl.CostEstimate(
-            flops=4 * total * seq * depth, bytes_accessed=4 * total * depth, transcendentals=0
-        ),
-        name="index_part",
-    )(iq, wide, keys)
+    )(latents, keys, iq, wide)
 
 
 def attend_kernel(
@@ -230,12 +274,17 @@
             seen = pos_ref[b] * rows + row <= mine
             bias[b * rows : (b + 1) * rows, :] = jnp.where(seen, 0.0, NEGATIVE)
 
-    def scores(first):
+    def scores(first, scr):
         def part(h):
             return q_ref[h][:, half * count : (half + 1) * count]
 
         weights = jnp.concatenate([part(first + h) for h in range(4)], axis=1)
-        return jnp.dot(lat_ref[...], weights, preferred_element_type=F32)
+        piece = seq // PIECES
+        for r in range(0, seq, piece):
+            scr[r : r + piece, :] = jnp.dot(
+                lat_ref[r : r + piece, :], weights, preferred_element_type=F32
+            )
+            yield
 
     def softmax(scr):
         scale = []
@@ -244,6 +293,7 @@
             for r in range(0, seq, run):
                 v = scr[r : r + run, tile] + bias[r : r + run, :]
                 top = v if top is None else jnp.maximum(top, v)
+                yield
             top = jnp.max(top, axis=0, keepdims=True)
             total = None
             for r in range(0, seq, run):
@@ -251,26 +301,35 @@
                 p = jnp.exp2((v - top) * (SCALE_ATTN * LOG2E))
                 scr[r : r + run, tile] = p
                 total = p if total is None else total + p
+                yield
             total = jnp.sum(total, axis=0, keepdims=True)
             scale.append(1.0 / (HEADS * total))
         for r in range(0, seq, run):
             acc[r : r + run, :] += (
                 scr[r : r + run, :lanes] * scale[0] + scr[r : r + run, lanes:] * scale[1]
             )
-
-    scr_a[...] = scores(0)
-    softmax(scr_b)
+            yield
+
+    def together(dots, vectors):
+        per = -(-5 * (seq // run) // PIECES)
+        for _ in dots:
+            for _ in range(per):
+                next(vectors, None)
+        for _ in vectors:
+            pass
+
+    together(scores(0, scr_a), softmax(scr_b))
 
     @pl.when(step == 0)
     def _():
         acc[...] = jnp.zeros_like(acc)
 
-    scr_b[...] = scores(4)
-    softmax(scr_a)
+    together(scores(4, scr_b), softmax(scr_a))
 
     @pl.when(step == pl.num_programs(0) - 1)
     def _():
-        softmax(scr_b)
+        for _ in softmax(scr_b):
+            pass
         both = jnp.transpose(acc[...])
         out = both[:count] + both[count:]
         out_ref[...] = out
@@ -507,10 +566,9 @@
     mine = jnp.sum(jnp.where(jnp.arange(n) == lax.axis_index("ctx"), block_pos, 0))
     pos_t = (mine * rows + local)[:, None]
 
-    lat, keys = gather(latents, index_keys, n)
+    lat, keys, own_i = gather(latents, index_keys, iq, wide, heads, n)
     lat = lat.reshape(seq, rank)
     keys = keys.reshape(seq, depth)
-    own_i = index_part(iq, wide, keys, heads)
     peers_i = swap(own_i, ranks)
     own_t, peers_t = [], []
     for k in range(2):

time: 142 us -> 137 us (0.965)
  Pallas kernels: 126 us -> 111 us
  waiting for transfers between devices: 0.01 us -> 11.1 us
    pallas_call x2, Pallas kernels: 48.4 us -> 32.5 us  [attend(): pl.pallas_call(functools.partial(attend_kernel, half, n), grid=(heads //...]
    ppermute x3, waiting for transfers between devices: 0.01 us -> 11.1 us  [swap(): lax.ppermute(value, 'head', [(i, (i + d) % ranks) for i in range(ranks)])]
    pallas_call x2 -> x1, Pallas kernels: 40.9 us -> 40.6 us  [gather(): pl.pallas_call(functools.partial(gather_kernel, n, heads), out_shape=(jax...]
  transfers between devices with their start and end apart: 3 -> 3, of which waited for: 0 -> 1; matrix products, arithmetic and copies ran while one was open for 2% -> 1% of each run, Pallas kernels for 34% -> 19%
where the time goes in v2:
time: 137 us; the launch traced here: 136 us
  Pallas kernels  111 us (81%)
  waiting for transfers between devices  11.1 us (8%)
  local copies, waits for them, and re-layouts  6.98 us (5%)
  other arithmetic  3.32 us (2%)
  starting transfers between devices  2.53 us (2%)
    pallas_call x1, Pallas kernels, gather(): pl.pallas_call(functools.partial(gather_kernel, n, heads), out_shape=(jax...  40.6 us
    pallas_call x2, Pallas kernels, attend(): pl.pallas_call(functools.partial(attend_kernel, half, n), grid=(heads //...  32.5 us
    pallas_call x2, Pallas kernels, back(): pl.pallas_call(functools.partial(back_kernel, heads, last), grid=(count /...  20.8 us
    pallas_call x1, Pallas kernels, scatter(): pl.pallas_call(functools.partial(scatter_kernel, n, ranks), out_shape=jax...  17.3 us
    ppermute x3, waiting for transfers between devices, swap(): lax.ppermute(value, 'head', [(i, (i + d) % ranks) for i in range(ranks)])  11.1 us
    unnamed x10, local copies, waits for them, and re-layouts  4.86 us
  transfers between devices with their start and end apart: 3, of which 1 were waited for; matrix products, arithmetic and copies ran while one was open for 1% of the time, Pallas kernels for 19%

profile of v2, /device:TPU:0, one launch (start us, length us, event | category | flops | bytes accessed | tf_op | source)
XLA Modules:
  0.0 136.5 jit_solution(8850122020796759433)
XLA Ops:
  0.6 0.7 broadcast_multiply_fusion
  1.4 0.1 copy.10
  1.5 0.1 broadcast_in_dim.10
  1.5 1.7 %copy.11.lat_ref = bf16[128,576]{1,0:T(8,128)(2,1)} copy(bf16[128,576]{0,1:T(8,128)(2,1)} %param.7) | data formatting | bytes 294912 | tf_op args[1]
  3.3 1.3 broadcast_multiply_fusion.1
  4.5 1.9 %broadcast_in_dim.20.w_ref = f32[4096,128]{1,0:T(8,128)} broadcast(f32[4096]{0:T(1024)S(1)} %broadcast_in_dim.10), dimensions={0} | broadcast | bytes 2113536 | tf_op jit(solution)/shard_map/broadcast_in_dim | solution.py:561
  6.5 40.6 %gather.1 = (bf16[16,128,576]{2,1,0:T(8,128)(2,1)}, bf16[16,128,128]{2,1,0:T(8,128)(2,1)}, f32[128,2048]{1,0:T(8,128)}) custom-call(bf16[128,576]{1,0:T(8,128)(2,1)} %copy.11.lat_ref, bf16[128,128]{1,0:T(8,128)(2,1)} %key_ref.1, bf16[4096,128]{1,0:T(8,128)(2,1)} %bitcast.11, f32[4096,128]{1,0:T(8,128)} %broadcast_in_dim.20.w_ref), custom_call_target="tpu_custom_call" | custom-call | tf_op jit(solution)/shard_map/gather/pallas_call | solution.py:235
  47.1 0.0 copy-start
  47.1 16.3 %attend.3 = (f32[64,2048]{1,0:T(8,128)}, bf16[64,2048]{1,0:T(8,128)(2,1)}) custom-call(bf16[32,576,128]{2,1,0:T(8,128)(2,1)} %bitcast.17, bf16[2048,576]{1,0:T(8,128)(2,1)} %bitcast.19, s32[16]{0:T(128)} %pos_ref.3, s32[1]{0:T(128)} %bitcast.6.mine_ref), custom_call_target="tpu_custom_call" | custom-call | flops 9663676416 | bytes 4718592 | tf_op jit(solution)/shard_map/attend/pallas_call | solution.py:345
  63.4 0.5 collective-permute-start.2
  63.9 0.0 copy-done
  63.9 1.5 %collective-permute-start = (f32[128,2048]{1,0:T(8,128)S(1)}, f32[128,2048]{1,0:T(8,128)S(1)}, u32[]{:S(2)}, u32[]{:S(2)}) collective-permute-start(f32[128,2048]{1,0:T(8,128)S(1)} %copy-done), channel_id=1, source_target_pairs={{0,1},{1,0},{2,3},{3,2},{4,5},{5,4},{6,7},{7,6},{8,9},{9,8},{10,11... | collective-permute-start | bytes 3145736 | tf_op jit(solution)/shard_map/ppermute | solution.py:548
  65.4 16.2 %attend.2 = (f32[64,2048]{1,0:T(8,128)}, bf16[64,2048]{1,0:T(8,128)(2,1)}) custom-call(bf16[32,576,128]{2,1,0:T(8,128)(2,1)} %bitcast.18, bf16[2048,576]{1,0:T(8,128)(2,1)} %bitcast.20, s32[16]{0:T(128)} %pos_ref.3, s32[1]{0:T(128)} %bitcast.6.mine_ref), custom_call_target="tpu_custom_call" | custom-call | flops 9663676416 | bytes 4718592 | tf_op jit(solution)/shard_map/attend/pallas_call | solution.py:345
  81.6 0.5 collective-permute-start.1
  82.8 0.6 iota_add_fusion.post_ref
  83.4 0.7 iota_add_fusion.1
  84.1 0.0 collective-permute-done.2
  84.1 0.0 copy-start.3
  84.1 11.1 %collective-permute-done = f32[128,2048]{1,0:T(8,128)S(1)} collective-permute-done((f32[128,2048]{1,0:T(8,128)S(1)}, f32[128,2048]{1,0:T(8,128)S(1)}, u32[]{:S(2)}, u32[]{:S(2)}) %collective-permute-start) | collective-permute-done | bytes 1048608 | tf_op jit(solution)/shard_map/ppermute | solution.py:548
  95.2 0.0 copy-start.1
  95.2 0.0 copy-done.3
  95.2 1.0 copy-done.1
  96.2 10.2 %back.2 = (f32[4096,128]{1,0:T(8,128)}, f32[128,2048]{1,0:T(8,128)}) custom-call(bf16[4096,128]{1,0:T(8,128)(2,1)} %bitcast.12, f32[4096,128]{1,0:T(8,128)} %broadcast_in_dim.20.w_ref, bf16[2048,128]{1,0:T(8,128)(2,1)} %bitcast.23, s32[128,1]{1,0:T(8,128)} %iota_add_fusion.post_ref, s32[1,2048]{1,0:T(1,128)} %bitcast.15, f32[1,128,2048]{2,1,0:T(8,128)} %bitcast.21, ...), custom_call_target="tpu_custom_call" | custom-call | flops 4294967296 | bytes 2097152 | tf_op jit(solution)/shard_map/back/pallas_call | solution.py:420
  106.5 0.0 collective-permute-done.1
  106.5 0.0 copy-start.2
  106.5 0.7 copy-done.2
  107.2 10.5 %back.3 = (f32[4096,128]{1,0:T(8,128)}, bf16[2048,128]{1,0:T(8,128)(2,1)}) custom-call(bf16[4096,128]{1,0:T(8,128)(2,1)} %bitcast.13, f32[4096,128]{1,0:T(8,128)} %broadcast_in_dim.20.w_ref, bf16[2048,128]{1,0:T(8,128)(2,1)} %bitcast.24, s32[128,1]{1,0:T(8,128)} %iota_add_fusion.post_ref, s32[1,2048]{1,0:T(1,128)} %bitcast.16, ...), custom_call_target="tpu_custom_call", output_to_operand_aliasing={{0}: (10, {})} | custom-call | flops 4294967296 | bytes 2097152 | tf_op jit(solution)/shard_map/back/pallas_call | solution.py:420
  117.7 17.3 %scatter.1 = f32[128,128]{1,0:T(8,128)} custom-call(bf16[4,2,2,128,128]{4,3,2,1,0:T(8,128)(2,1)} %bitcast.14), custom_call_target="tpu_custom_call" | custom-call | tf_op jit(solution)/shard_map/scatter/pallas_call | solution.py:522
  135.0 1.5 %copy.14 = f32[128,128]{1,0:T(8,128)} copy(f32[128,128]{1,0:T(8,128)} %scatter.1) | data formatting | bytes 131072
Async XLA Ops:
  47.1 16.8 %copy-start = (f32[128,2048]{1,0:T(8,128)S(1)}, f32[128,2048]{1,0:T(8,128)}, u32[]{:S(2)}) copy-start(f32[128,2048]{1,0:T(8,128)} %get-tuple-element.14.rest_1_) | copy-start | bytes 3145732
  63.4 20.7 %collective-permute-start.2 = (bf16[64,2048]{1,0:T(8,128)(2,1)}, bf16[64,2048]{1,0:T(8,128)(2,1)S(1)}, u32[]{:S(2)}, u32[]{:S(2)}) collective-permute-start(bf16[64,2048]{1,0:T(8,128)(2,1)} %get-tuple-element.19), channel_id=1, source_target_pairs={{0,1},{1,0},{2,3},{3,2},{4,5},{5,4},{6,7},{7,6},{8,9},{9,8},{10,11... | collective-permute-start | bytes 786440 | tf_op jit(solution)/shard_map/ppermute | solution.py:548
  63.9 31.3 %collective-permute-start = (f32[128,2048]{1,0:T(8,128)S(1)}, f32[128,2048]{1,0:T(8,128)S(1)}, u32[]{:S(2)}, u32[]{:S(2)}) collective-permute-start(f32[128,2048]{1,0:T(8,128)S(1)} %copy-done), channel_id=1, source_target_pairs={{0,1},{1,0},{2,3},{3,2},{4,5},{5,4},{6,7},{7,6},{8,9},{9,8},{10,11... | collective-permute-start | bytes 3145736 | tf_op jit(solution)/shard_map/ppermute | solution.py:548
  81.6 24.8 %collective-permute-start.1 = (bf16[64,2048]{1,0:T(8,128)(2,1)}, bf16[64,2048]{1,0:T(8,128)(2,1)S(1)}, u32[]{:S(2)}, u32[]{:S(2)}) collective-permute-start(bf16[64,2048]{1,0:T(8,128)(2,1)} %get-tuple-element.17), channel_id=1, source_target_pairs={{0,1},{1,0},{2,3},{3,2},{4,5},{5,4},{6,7},{7,6},{8,9},{9,8},{10,11... | collective-permute-start | bytes 786440 | tf_op jit(solution)/shard_map/ppermute | solution.py:548
  84.1 11.1 %copy-start.3 = (bf16[64,2048]{1,0:T(8,128)(2,1)}, bf16[64,2048]{1,0:T(8,128)(2,1)S(1)}, u32[]{:S(2)}) copy-start(bf16[64,2048]{1,0:T(8,128)(2,1)S(1)} %collective-permute-done.2) | copy-start | bytes 786436
  95.2 1.0 copy-start.1
  106.5 0.7 copy-start.2

commit v3 on v2

--- a/solution.py
+++ b/solution.py
@@ -49,7 +49,6 @@
     z, x, c, a = place(n)
     y = lax.axis_index("head")
     other_y = y + 1 - 2 * (y % 2)
-    up, down = z + 1 < a, z > 0
     partner = at(z, x, 1 - c)
     barrier = pltpu.get_barrier_semaphore()
 
@@ -60,13 +59,8 @@
     greet(ctx=partner)
     greet(head=other_y)
 
-    @pl.when(up)
-    def _():
-        greet(ctx=at(z + 1, x, c))
-
-    @pl.when(down)
-    def _():
-        greet(ctx=at(z - 1, x, c))
+    for d in range(1, a):
+        greet(ctx=at((z + d) % a, x, c))
 
     me = at(z, x, c)
     owns = []
@@ -74,7 +68,7 @@
         own = pltpu.make_async_copy(src, dst.at[me], own_sem.at[k])
         own.start()
         owns.append(own)
-    pl.semaphore_wait(barrier, 3 + up.astype(jnp.int32) + down.astype(jnp.int32))
+    pl.semaphore_wait(barrier, 2 + a)
 
     rows = lat_ref.shape[0]
     part = rows // 2
@@ -97,23 +91,14 @@
         return copy(k, slot, 1, first, ctx=at(z, 1 - x, c))
 
     def to_y(k, slot):
-        return copy(k, slot, 4, False, head=other_y)
+        return copy(k, slot, 2, False, head=other_y)
 
     def arrived(k, slot):
         to_core(k, slot).wait_recv()
 
-    def line(k, slot, first, side, act):
-        if side >= 0:
-
-            @pl.when(up)
-            def _():
-                act(copy(k, slot, 2, first, ctx=at(z + 1, x, c)))
-
-        if side <= 0:
-
-            @pl.when(down)
-            def _():
-                act(copy(k, slot, 3, first, ctx=at(z - 1, x, c)))
+    def line(k, slot, act):
+        for d in range(1, a):
+            act(copy(k, slot, 4 + d, True, ctx=at((z + d) % a, x, c)))
 
     def sides(d, act):
         for side in (1, -1) if d > 0 else (0,):
@@ -134,7 +119,8 @@
             for k in ks:
                 if wait and d > 0:
                     arrived(k, slot)
-                line(k, slot, d == 0, side, act)
+                if d == 0:
+                    line(k, slot, act)
             crossing = 0 if ks == (0,) else mine
             act(to_x(crossing, slot, d == 0))
             for k in ks:
@@ -154,24 +140,25 @@
         sides(d, go)
 
     column((0,), 0, True, start)
-    column((1, 2), 0, True, start)
     for d in range(1, a):
         column((0,), d, True, start)
-        crossed(0, d - 1, True, start, False)
-    crossed(0, a - 1, True, start, False)
+    column((1, 2), 0, True, start)
+    for d in range(a):
+        crossed(0, d, True, start, False)
 
     owns[0].wait()
     for zs in range(a):
         for xs in range(2):
             arrived(0, at(zs, xs, 1 - c))
 
-    def stage(d):
-        if d < a:
-            column((1, 2), d, True, start)
+    stages = []
+    for d in range(a + 2):
+        if 1 <= d < a:
+            stages.append(functools.partial(column, (1, 2), d, True, start))
         if 1 <= d <= a:
-            crossed(mine, d - 1, True, start, True)
+            stages.append(functools.partial(crossed, mine, d - 1, True, start, True))
         if 2 <= d:
-            crossed(others, d - 2, True, start, False)
+            stages.append(functools.partial(crossed, others, d - 2, True, start, False))
 
     depth = iq_ref.shape[1]
     m = ITOK * heads
@@ -206,11 +193,14 @@
         return 0
 
     chunks = iq_ref.shape[0] // m
-    cut = [chunks * d // (a + 2) for d in range(a + 3)]
-    for d in range(a + 2):
-        lax.fori_loop(cut[d], cut[d + 1], index_chunk, 0)
-        if d + 1 < a + 2:
-            stage(d + 1)
+    lead = chunks // 4
+    count = len(stages)
+    cut = [0] + [lead + (chunks - lead) * d // count for d in range(count)] + [chunks]
+    for d in range(count + 1):
+        if cut[d + 1] > cut[d]:
+            lax.fori_loop(cut[d], cut[d + 1], index_chunk, 0)
+        if d < count:
+            stages[d]()
 
     owns[1].wait()
     for zs in range(a):
@@ -244,7 +234,7 @@
         scratch_shapes=[
             pltpu.VMEM((m, 4 * rows), F32),
             pltpu.VMEM((m, 4 * rows), F32),
-            pltpu.SemaphoreType.DMA((3, n, 5)),
+            pltpu.SemaphoreType.DMA((3, n, 4 + n // 4)),
             pltpu.SemaphoreType.DMA((3, n)),
             pltpu.SemaphoreType.DMA((2,)),
         ],
@@ -364,9 +354,9 @@
         ],
         compiler_params=pltpu.CompilerParams(vmem_limit_bytes=VMEM_LIMIT),
         cost_estimate=pl.CostEstimate(
-            flops=4 * count * heads * seq * depth,
+            flops=count * heads * seq * depth // 8,
             bytes_accessed=4 * count * heads * depth,
-            transcendentals=count * heads * seq,
+            transcendentals=0,
         ),
         name="attend",
     )(q, lat, block_pos, mine)

time: 137 us -> 129 us (0.942)
  waiting for transfers between devices: 11.1 us -> 0.01 us
  Pallas kernels: 111 us -> 115 us
    ppermute x3, waiting for transfers between devices: 11.1 us -> 0.01 us  [swap(): lax.ppermute(value, 'head', [(i, (i + d) % ranks) for i in range(ranks)])]
    pallas_call x1, Pallas kernels: 17.3 us -> 19.5 us  [scatter(): pl.pallas_call(functools.partial(scatter_kernel, n, ranks), out_shape=jax...]
  transfers between devices with their start and end apart: 3 -> 3, of which waited for: 1 -> 0; matrix products, arithmetic and copies ran while one was open for 1% -> 2% of each run, Pallas kernels for 19% -> 33%
where the time goes in v3:
time: 129 us; the launch traced here: 128 us
  Pallas kernels  115 us (89%)
  local copies, waits for them, and re-layouts  7.06 us (5%)
  other arithmetic  2.66 us (2%)
  starting transfers between devices  2.56 us (2%)
  between operations  1.34 us (1%)
    pallas_call x1, Pallas kernels, gather(): pl.pallas_call(functools.partial(gather_kernel, n, heads), out_shape=(jax...  41.9 us
    pallas_call x2, Pallas kernels, attend(): pl.pallas_call(functools.partial(attend_kernel, half, n), grid=(heads //...  32.6 us
    pallas_call x2, Pallas kernels, back(): pl.pallas_call(functools.partial(back_kernel, heads, last), grid=(count /...  20.8 us
    pallas_call x1, Pallas kernels, scatter(): pl.pallas_call(functools.partial(scatter_kernel, n, ranks), out_shape=jax...  19.5 us
    unnamed x10, local copies, waits for them, and re-layouts  4.95 us
  transfers between devices with their start and end apart: 3, of which 0 were waited for; matrix products, arithmetic and copies ran while one was open for 2% of the time, Pallas kernels for 33%

profile of v3, /device:TPU:0, one launch (start us, length us, event | category | flops | bytes accessed | tf_op | source)
XLA Modules:
  0.0 128.4 jit_solution(3154600644498379891)
XLA Ops:
  0.6 0.7 broadcast_multiply_fusion
  1.4 0.1 copy.10
  1.4 0.1 broadcast_in_dim.10
  1.5 1.7 %copy.11.lat_ref = bf16[128,576]{1,0:T(8,128)(2,1)} copy(bf16[128,576]{0,1:T(8,128)(2,1)} %param.7) | data formatting | bytes 294912 | tf_op args[1]
  3.3 1.9 %broadcast_in_dim.20.w_ref = f32[4096,128]{1,0:T(8,128)} broadcast(f32[4096]{0:T(1024)S(1)} %broadcast_in_dim.10), dimensions={0} | broadcast | bytes 2113536 | tf_op jit(solution)/shard_map/broadcast_in_dim | solution.py:551
  5.2 0.0 copy-start
  5.2 41.9 %gather.1 = (bf16[16,128,576]{2,1,0:T(8,128)(2,1)}, bf16[16,128,128]{2,1,0:T(8,128)(2,1)}, f32[128,2048]{1,0:T(8,128)}) custom-call(bf16[128,576]{1,0:T(8,128)(2,1)} %copy.11.lat_ref, bf16[128,128]{1,0:T(8,128)(2,1)} %key_ref.1, bf16[4096,128]{1,0:T(8,128)(2,1)} %bitcast.15, f32[4096,128]{1,0:T(8,128)} %broadcast_in_dim.20.w_ref), custom_call_target="tpu_custom_call" | custom-call | tf_op jit(solution)/shard_map/gather/pallas_call | solution.py:225
  47.1 0.6 collective-permute-start
  47.7 0.0 copy-done
  47.7 0.6 broadcast_multiply_fusion.1
  48.3 16.2 %attend.3 = (f32[64,2048]{1,0:T(8,128)}, bf16[64,2048]{1,0:T(8,128)(2,1)}) custom-call(bf16[32,576,128]{2,1,0:T(8,128)(2,1)} %bitcast.11, bf16[2048,576]{1,0:T(8,128)(2,1)} %bitcast.13, s32[16]{0:T(128)} %pos_ref.3, s32[1]{0:T(128)} %bitcast.6.mine_ref), custom_call_target="tpu_custom_call" | custom-call | flops 301989888 | bytes 4718592 | tf_op jit(solution)/shard_map/attend/pallas_call | solution.py:335
  64.5 1.5 %collective-permute-start.2 = (bf16[64,2048]{1,0:T(8,128)(2,1)}, bf16[64,2048]{1,0:T(8,128)(2,1)S(1)}, u32[]{:S(2)}, u32[]{:S(2)}) collective-permute-start(bf16[64,2048]{1,0:T(8,128)(2,1)} %get-tuple-element.19), channel_id=1, source_target_pairs={{0,1},{1,0},{2,3},{3,2},{4,5},{5,4},{6,7},{7,6},{8,9},{9,8},{10,11... | collective-permute-start | bytes 786440 | tf_op jit(solution)/shard_map/ppermute | solution.py:538
  66.0 16.4 %attend.2 = (f32[64,2048]{1,0:T(8,128)}, bf16[64,2048]{1,0:T(8,128)(2,1)}) custom-call(bf16[32,576,128]{2,1,0:T(8,128)(2,1)} %bitcast.12, bf16[2048,576]{1,0:T(8,128)(2,1)} %bitcast.14, s32[16]{0:T(128)} %pos_ref.3, s32[1]{0:T(128)} %bitcast.6.mine_ref), custom_call_target="tpu_custom_call" | custom-call | flops 301989888 | bytes 4718592 | tf_op jit(solution)/shard_map/attend/pallas_call | solution.py:335
  82.4 0.5 collective-permute-start.1
  83.6 0.6 iota_add_fusion.post_ref
  84.2 0.7 iota_add_fusion.1
  84.9 0.0 collective-permute-done.2
  84.9 0.0 copy-start.3
  84.9 0.0 collective-permute-done
  84.9 0.0 copy-start.1
  84.9 0.7 copy-done.3
  85.6 0.4 copy-done.1
  86.0 10.2 %back.2 = (f32[4096,128]{1,0:T(8,128)}, f32[128,2048]{1,0:T(8,128)}) custom-call(bf16[4096,128]{1,0:T(8,128)(2,1)} %bitcast.16, f32[4096,128]{1,0:T(8,128)} %broadcast_in_dim.20.w_ref, bf16[2048,128]{1,0:T(8,128)(2,1)} %bitcast.23, s32[128,1]{1,0:T(8,128)} %iota_add_fusion.post_ref, s32[1,2048]{1,0:T(1,128)} %bitcast.19, f32[1,128,2048]{2,1,0:T(8,128)} %bitcast.21, ...), custom_call_target="tpu_custom_call" | custom-call | flops 4294967296 | bytes 2097152 | tf_op jit(solution)/shard_map/back/pallas_call | solution.py:410
  96.2 0.0 collective-permute-done.1
  96.2 0.0 copy-start.2
  96.2 0.7 copy-done.2
  96.9 10.5 %back.3 = (f32[4096,128]{1,0:T(8,128)}, bf16[2048,128]{1,0:T(8,128)(2,1)}) custom-call(bf16[4096,128]{1,0:T(8,128)(2,1)} %bitcast.17, f32[4096,128]{1,0:T(8,128)} %broadcast_in_dim.20.w_ref, bf16[2048,128]{1,0:T(8,128)(2,1)} %bitcast.24, s32[128,1]{1,0:T(8,128)} %iota_add_fusion.post_ref, s32[1,2048]{1,0:T(1,128)} %bitcast.20, ...), custom_call_target="tpu_custom_call", output_to_operand_aliasing={{0}: (10, {})} | custom-call | flops 4294967296 | bytes 2097152 | tf_op jit(solution)/shard_map/back/pallas_call | solution.py:410
  107.4 19.5 %scatter.1 = f32[128,128]{1,0:T(8,128)} custom-call(bf16[4,2,2,128,128]{4,3,2,1,0:T(8,128)(2,1)} %bitcast.18), custom_call_target="tpu_custom_call" | custom-call | tf_op jit(solution)/shard_map/scatter/pallas_call | solution.py:512
  126.9 1.5 %copy.14 = f32[128,128]{1,0:T(8,128)} copy(f32[128,128]{1,0:T(8,128)} %scatter.1) | data formatting | bytes 131072
Async XLA Ops:
  5.2 42.5 %copy-start = (s32[16]{0:T(128)S(1)}, s32[16]{0:T(128)}, u32[]{:S(2)}) copy-start(s32[16]{0:T(128)} %pos_ref.3) | copy-start | bytes 196
  47.1 37.8 %collective-permute-start = (f32[128,2048]{1,0:T(8,128)}, f32[128,2048]{1,0:T(8,128)S(1)}, u32[]{:S(2)}, u32[]{:S(2)}) collective-permute-start(f32[128,2048]{1,0:T(8,128)} %get-tuple-element.14.rest_1_), channel_id=1, source_target_pairs={{0,1},{1,0},{2,3},{3,2},{4,5},{5,4},{6,7},{7,6},{8,9},{9,8},{10,11... | collective-permute-start | bytes 3145736 | tf_op jit(solution)/shard_map/ppermute | solution.py:538
  64.5 20.4 %collective-permute-start.2 = (bf16[64,2048]{1,0:T(8,128)(2,1)}, bf16[64,2048]{1,0:T(8,128)(2,1)S(1)}, u32[]{:S(2)}, u32[]{:S(2)}) collective-permute-start(bf16[64,2048]{1,0:T(8,128)(2,1)} %get-tuple-element.19), channel_id=1, source_target_pairs={{0,1},{1,0},{2,3},{3,2},{4,5},{5,4},{6,7},{7,6},{8,9},{9,8},{10,11... | collective-permute-start | bytes 786440 | tf_op jit(solution)/shard_map/ppermute | solution.py:538
  82.4 13.8 %collective-permute-start.1 = (bf16[64,2048]{1,0:T(8,128)(2,1)}, bf16[64,2048]{1,0:T(8,128)(2,1)S(1)}, u32[]{:S(2)}, u32[]{:S(2)}) collective-permute-start(bf16[64,2048]{1,0:T(8,128)(2,1)} %get-tuple-element.17), channel_id=1, source_target_pairs={{0,1},{1,0},{2,3},{3,2},{4,5},{5,4},{6,7},{7,6},{8,9},{9,8},{10,11... | collective-permute-start | bytes 786440 | tf_op jit(solution)/shard_map/ppermute | solution.py:538
  84.9 0.7 copy-start.3
  84.9 1.1 copy-start.1
  96.2 0.7 copy-start.2

commit v4 on v3

--- a/solution.py
+++ b/solution.py
@@ -177,7 +177,9 @@
                 acc = None
                 for g in range(0, heads, 8):
                     r = t * heads + g
-                    term = jnp.maximum(scr[r : r + 8, :], 0.0) * w[r : r + 8, 0:1]
+                    term = jnp.maximum(scr[r : r + 8, :], 0.0) * jnp.concatenate(
+                        [w[r : r + 8, :]] * (width // 128), axis=1
+                    )
                     acc = term if acc is None else acc + term
                 sums.append(jnp.sum(acc, axis=0, keepdims=True))
             out[:, p * width : (p + 1) * width] = jnp.concatenate(sums, axis=0)
@@ -385,7 +387,8 @@
     for t in range(TOK):
         for g in range(0, heads, 8):
             r = t * heads + g
-            value = dscr[t : t + 1, :] * w_ref[r : r + 8, 0:1]
+            wide = jnp.concatenate([w_ref[r : r + 8, :]] * (dscr.shape[1] // 128), axis=1)
+            value = dscr[t : t + 1, :] * wide
             coef[r : r + 8, :] = jnp.where(scr[r : r + 8, :] > 0.0, value, 0.0).astype(BF16)
     gq_ref[...] = jnp.dot(coef[...], key_ref[...], preferred_element_type=F32)
     acc[...] += lax.dot_general(

time: 129 us -> 129 us (level)
  no operation moved by 1% of the time
where the time goes in v4:
time: 129 us; the launch traced here: 128 us
  Pallas kernels  115 us (89%)
  local copies, waits for them, and re-layouts  7.06 us (5%)
  other arithmetic  2.66 us (2%)
  starting transfers between devices  2.57 us (2%)
  between operations  1.34 us (1%)
    pallas_call x1, Pallas kernels, gather(): pl.pallas_call(functools.partial(gather_kernel, n, heads), out_shape=(jax...  41.9 us
    pallas_call x2, Pallas kernels, attend(): pl.pallas_call(functools.partial(attend_kernel, half, n), grid=(heads //...  32.6 us
    pallas_call x2, Pallas kernels, back(): pl.pallas_call(functools.partial(back_kernel, heads, last), grid=(count /...  20.7 us
    pallas_call x1, Pallas kernels, scatter(): pl.pallas_call(functools.partial(scatter_kernel, n, ranks), out_shape=jax...  19.4 us
    unnamed x10, local copies, waits for them, and re-layouts  4.95 us
  transfers between devices with their start and end apart: 3, of which 0 were waited for; matrix products, arithmetic and copies ran while one was open for 2% of the time, Pallas kernels for 33%

profile of v4, /device:TPU:0, one launch (start us, length us, event | category | flops | bytes accessed | tf_op | source)
XLA Modules:
  0.0 128.3 jit_solution(13392047118395058436)
XLA Ops:
  0.6 0.7 broadcast_multiply_fusion
  1.4 0.1 copy.10
  1.4 0.1 broadcast_in_dim.10
  1.5 1.7 %copy.11.lat_ref = bf16[128,576]{1,0:T(8,128)(2,1)} copy(bf16[128,576]{0,1:T(8,128)(2,1)} %param.7) | data formatting | bytes 294912 | tf_op args[1]
  3.3 1.9 %broadcast_in_dim.20.w_ref = f32[4096,128]{1,0:T(8,128)} broadcast(f32[4096]{0:T(1024)S(1)} %broadcast_in_dim.10), dimensions={0} | broadcast | bytes 2113536 | tf_op jit(solution)/shard_map/broadcast_in_dim | solution.py:554
  5.2 0.0 copy-start
  5.2 41.9 %gather.1 = (bf16[16,128,576]{2,1,0:T(8,128)(2,1)}, bf16[16,128,128]{2,1,0:T(8,128)(2,1)}, f32[128,2048]{1,0:T(8,128)}) custom-call(bf16[128,576]{1,0:T(8,128)(2,1)} %copy.11.lat_ref, bf16[128,128]{1,0:T(8,128)(2,1)} %key_ref.1, bf16[4096,128]{1,0:T(8,128)(2,1)} %bitcast.15, f32[4096,128]{1,0:T(8,128)} %broadcast_in_dim.20.w_ref), custom_call_target="tpu_custom_call" | custom-call | tf_op jit(solution)/shard_map/gather/pallas_call | solution.py:227
  47.1 0.6 collective-permute-start
  47.7 0.0 copy-done
  47.7 0.6 broadcast_multiply_fusion.1
  48.3 16.2 %attend.3 = (f32[64,2048]{1,0:T(8,128)}, bf16[64,2048]{1,0:T(8,128)(2,1)}) custom-call(bf16[32,576,128]{2,1,0:T(8,128)(2,1)} %bitcast.11, bf16[2048,576]{1,0:T(8,128)(2,1)} %bitcast.13, s32[16]{0:T(128)} %pos_ref.3, s32[1]{0:T(128)} %bitcast.6.mine_ref), custom_call_target="tpu_custom_call" | custom-call | flops 301989888 | bytes 4718592 | tf_op jit(solution)/shard_map/attend/pallas_call | solution.py:337
  64.5 1.5 %collective-permute-start.2 = (bf16[64,2048]{1,0:T(8,128)(2,1)}, bf16[64,2048]{1,0:T(8,128)(2,1)S(1)}, u32[]{:S(2)}, u32[]{:S(2)}) collective-permute-start(bf16[64,2048]{1,0:T(8,128)(2,1)} %get-tuple-element.19), channel_id=1, source_target_pairs={{0,1},{1,0},{2,3},{3,2},{4,5},{5,4},{6,7},{7,6},{8,9},{9,8},{10,11... | collective-permute-start | bytes 786440 | tf_op jit(solution)/shard_map/ppermute | solution.py:541
  66.0 16.4 %attend.2 = (f32[64,2048]{1,0:T(8,128)}, bf16[64,2048]{1,0:T(8,128)(2,1)}) custom-call(bf16[32,576,128]{2,1,0:T(8,128)(2,1)} %bitcast.12, bf16[2048,576]{1,0:T(8,128)(2,1)} %bitcast.14, s32[16]{0:T(128)} %pos_ref.3, s32[1]{0:T(128)} %bitcast.6.mine_ref), custom_call_target="tpu_custom_call" | custom-call | flops 301989888 | bytes 4718592 | tf_op jit(solution)/shard_map/attend/pallas_call | solution.py:337
  82.4 0.5 collective-permute-start.1
  83.6 0.6 iota_add_fusion.post_ref
  84.2 0.7 iota_add_fusion.1
  84.9 0.0 collective-permute-done.2
  84.9 0.0 copy-start.3
  84.9 0.0 collective-permute-done
  84.9 0.0 copy-start.1
  84.9 0.7 copy-done.3
  85.6 0.4 copy-done.1
  86.0 10.2 %back.2 = (f32[4096,128]{1,0:T(8,128)}, f32[128,2048]{1,0:T(8,128)}) custom-call(bf16[4096,128]{1,0:T(8,128)(2,1)} %bitcast.16, f32[4096,128]{1,0:T(8,128)} %broadcast_in_dim.20.w_ref, bf16[2048,128]{1,0:T(8,128)(2,1)} %bitcast.23, s32[128,1]{1,0:T(8,128)} %iota_add_fusion.post_ref, s32[1,2048]{1,0:T(1,128)} %bitcast.19, f32[1,128,2048]{2,1,0:T(8,128)} %bitcast.21, ...), custom_call_target="tpu_custom_call" | custom-call | flops 4294967296 | bytes 2097152 | tf_op jit(solution)/shard_map/back/pallas_call | solution.py:413
  96.2 0.0 collective-permute-done.1
  96.2 0.0 copy-start.2
  96.2 0.7 copy-done.2
  96.9 10.5 %back.3 = (f32[4096,128]{1,0:T(8,128)}, bf16[2048,128]{1,0:T(8,128)(2,1)}) custom-call(bf16[4096,128]{1,0:T(8,128)(2,1)} %bitcast.17, f32[4096,128]{1,0:T(8,128)} %broadcast_in_dim.20.w_ref, bf16[2048,128]{1,0:T(8,128)(2,1)} %bitcast.24, s32[128,1]{1,0:T(8,128)} %iota_add_fusion.post_ref, s32[1,2048]{1,0:T(1,128)} %bitcast.20, ...), custom_call_target="tpu_custom_call", output_to_operand_aliasing={{0}: (10, {})} | custom-call | flops 4294967296 | bytes 2097152 | tf_op jit(solution)/shard_map/back/pallas_call | solution.py:413
  107.4 19.4 %scatter.1 = f32[128,128]{1,0:T(8,128)} custom-call(bf16[4,2,2,128,128]{4,3,2,1,0:T(8,128)(2,1)} %bitcast.18), custom_call_target="tpu_custom_call" | custom-call | tf_op jit(solution)/shard_map/scatter/pallas_call | solution.py:515
  126.8 1.5 %copy.14 = f32[128,128]{1,0:T(8,128)} copy(f32[128,128]{1,0:T(8,128)} %scatter.1) | data formatting | bytes 131072
Async XLA Ops:
  5.2 42.5 %copy-start = (s32[16]{0:T(128)S(1)}, s32[16]{0:T(128)}, u32[]{:S(2)}) copy-start(s32[16]{0:T(128)} %pos_ref.3) | copy-start | bytes 196
  47.1 37.8 %collective-permute-start = (f32[128,2048]{1,0:T(8,128)}, f32[128,2048]{1,0:T(8,128)S(1)}, u32[]{:S(2)}, u32[]{:S(2)}) collective-permute-start(f32[128,2048]{1,0:T(8,128)} %get-tuple-element.14.rest_1_), channel_id=1, source_target_pairs={{0,1},{1,0},{2,3},{3,2},{4,5},{5,4},{6,7},{7,6},{8,9},{9,8},{10,11... | collective-permute-start | bytes 3145736 | tf_op jit(solution)/shard_map/ppermute | solution.py:541
  64.5 20.4 %collective-permute-start.2 = (bf16[64,2048]{1,0:T(8,128)(2,1)}, bf16[64,2048]{1,0:T(8,128)(2,1)S(1)}, u32[]{:S(2)}, u32[]{:S(2)}) collective-permute-start(bf16[64,2048]{1,0:T(8,128)(2,1)} %get-tuple-element.19), channel_id=1, source_target_pairs={{0,1},{1,0},{2,3},{3,2},{4,5},{5,4},{6,7},{7,6},{8,9},{9,8},{10,11... | collective-permute-start | bytes 786440 | tf_op jit(solution)/shard_map/ppermute | solution.py:541
  82.4 13.8 %collective-permute-start.1 = (bf16[64,2048]{1,0:T(8,128)(2,1)}, bf16[64,2048]{1,0:T(8,128)(2,1)S(1)}, u32[]{:S(2)}, u32[]{:S(2)}) collective-permute-start(bf16[64,2048]{1,0:T(8,128)(2,1)} %get-tuple-element.17), channel_id=1, source_target_pairs={{0,1},{1,0},{2,3},{3,2},{4,5},{5,4},{6,7},{7,6},{8,9},{9,8},{10,11... | collective-permute-start | bytes 786440 | tf_op jit(solution)/shard_map/ppermute | solution.py:541
  84.9 0.7 copy-start.3
  84.9 1.1 copy-start.1
  96.2 0.7 copy-start.2
